TPU v7x, 32 devices: a whole 2x2x4 slice. The times are simulated.
32 devices in a mesh: dp: 2 (over x), ctx: 16 (over z, y, core).
Axes of the slice: x: 2, y: 2, z: 4, core: 2. Of those that a mesh axis runs over, the one named last changes fastest.
Arguments:
- hidden: bfloat16 [16384, 4096], P(('dp', 'ctx')), parts along dimension 0, may hold values from -24 to 24
- dest: int32 [16384], P(('dp', 'ctx')), parts along dimension 0, may hold values from 0 to 8191, as said below
- doc_ids: int32 [16384], P('dp'), parts along dimension 0, may hold values from 0 to 63, never falling along the last dimension, each value on 1 to 1024 neighbouring positions
- w_query: bfloat16 [4096, 2048], P('ctx'), may hold values from -0.09375 to 0.09375
- key_weight: bfloat16 [4096, 512], P('ctx'), may hold values from -0.09375 to 0.09375
- value_weight: bfloat16 [4096, 512], P('ctx'), may hold values from -0.09375 to 0.09375
Outputs:
- attended: bfloat16 [16384, 2048], P(('dp', 'ctx')), parts along dimension 0
There are 2 independent parts, one for each index of `dp`. A program takes and returns all parts, laid end to end along the dimension named above; an argument that names none is the same for every part. Nothing has to cross between parts.
Inputs may be any that keep to these rules, and one draw needn't show every extreme that they name: `dest`: A permutation. Each block of 512 loader rows sends at most 64 rows to one block of 512 context positions, exactly 64 to some.
All inputs are finite; a program needn't handle non-finite values.
Results may differ from a plain program's by a relative error of at most 0.024.
Values may be sent and summed in bfloat16 or wider, within the bound.
No kernel may reach another device: no remote copies, remote signals or barrier semaphores. Data moves between devices by JAX's collectives and lax.ppermute only.
A program may use at most 128 MiB of HBM per device.

v0:
```python
import functools

import jax
import jax.numpy as jnp
from jax import lax
from jax.experimental import pallas as pl
from jax.experimental.pallas import tpu as pltpu
from jax.sharding import PartitionSpec as P


HEAD = 128
ROPE_BASE = 500000.0 * 16.0 ** (128.0 / 126.0)
MASKED = -1e30
QT = 128
VMEM_LIMIT = 56 * 1024 * 1024


def params(n=1):
    return pltpu.CompilerParams(
        dimension_semantics=("arbitrary",) * n, vmem_limit_bytes=VMEM_LIMIT
    )


def project_kernel(koff, x0, x1, slots, *refs):
    *ws, out, y = refs
    i = pl.program_id(0)
    half = lax.rem(i, 2)
    bm = x0.shape[0]
    kk = ws[0].shape[0] // 2
    n = ws[0].shape[1]

    def compute(x):
        acc = jnp.zeros((bm, n), jnp.float32)
        for k, w in enumerate(ws):
            for h in range(2):
                off = pl.multiple_of(koff[2 * k + h], kk)
                acc = acc + jnp.dot(
                    x[:, pl.ds(off, kk)],
                    w[h * kk : (h + 1) * kk, :],
                    preferred_element_type=jnp.float32,
                )
        y[pl.ds(pl.multiple_of(half * bm, bm), bm), :] = acc.astype(y.dtype)

    @pl.when(i < 2)
    def _():
        compute(x0)

    @pl.when(i >= 2)
    def _():
        compute(x1)

    @pl.when(half == 1)
    def _():
        chips, _, per, _ = out.shape
        rows = y.shape[0]
        row_slot = slots[0]
        step = max(1, 256 // per)
        for a in range(0, chips, step):
            ids = lax.broadcasted_iota(jnp.int32, (step * per, rows), 0) + a * per
            pick = jnp.where(ids == row_slot, 1.0, 0.0).astype(y.dtype)
            part = jnp.dot(pick, y[...], preferred_element_type=jnp.float32)
            out[a : a + step, 0] = part.astype(out.dtype).reshape(step, per, n)


def project(x0, x1, slots, ws, koff, per):
    rows, width = x0.shape
    n = ws[0].shape[1]
    chips = len(ws)
    bm = rows // 2
    grid_spec = pltpu.PrefetchScalarGridSpec(
        num_scalar_prefetch=1,
        grid=(4,),
        in_specs=[
            pl.BlockSpec((bm, width), lambda i, s: (jnp.minimum(i, 1), 0)),
            pl.BlockSpec((bm, width), lambda i, s: (jnp.maximum(i - 2, 0), 0)),
            pl.BlockSpec((1, 1, rows), lambda i, s: (i // 2, 0, 0)),
        ]
        + [pl.BlockSpec(w.shape, lambda i, s: (0, 0)) for w in ws],
        out_specs=pl.BlockSpec((chips, 1, per, n), lambda i, s: (0, i // 2, 0, 0)),
        scratch_shapes=[pltpu.VMEM((rows, n), x0.dtype)],
    )
    return pl.pallas_call(
        project_kernel,
        grid_spec=grid_spec,
        out_shape=jax.ShapeDtypeStruct((chips, 2, per, n), x0.dtype),
        compiler_params=params(),
        name="project",
    )(koff, x0, x1, slots, *ws)


def unpack_rows(got, target, rows):
    slots = got.shape[0]
    ids = lax.broadcasted_iota(jnp.int32, (rows, slots), 0)
    pick = jnp.where(ids == target, 1.0, 0.0).astype(got.dtype)
    return jnp.dot(pick, got, preferred_element_type=jnp.float32)


def rotated(v, cosine, sine):
    return v * cosine + pltpu.roll(v, HEAD // 2, 1) * sine


def keys_kernel(core, got, target, cosine, sine, first, second):
    v = unpack_rows(got[...].reshape(-1, got.shape[-1]), target[0], first.shape[0])
    k = rotated(v[:, :HEAD], cosine[...], sine[...])
    for e, out in enumerate((first, second)):

        @pl.when(pl.program_id(0) == e)
        def _(out=out):
            out[:, :HEAD] = k.astype(out.dtype)
            out[:, HEAD:] = v[:, HEAD:].astype(out.dtype)


def unpack_keys(core, got, target, cosine, sine, rows):
    chips, _, _, cap, n = got.shape
    grid_spec = pltpu.PrefetchScalarGridSpec(
        num_scalar_prefetch=1,
        grid=(2,),
        in_specs=[
            pl.BlockSpec((chips, 2, 1, cap, n), lambda e, s: (0, 0, e ^ s[0], 0, 0)),
            pl.BlockSpec((1, 1, chips * 2 * cap), lambda e, s: (e ^ s[0], 0, 0)),
            pl.BlockSpec((rows, HEAD), lambda e, s: (e, 0)),
            pl.BlockSpec((rows, HEAD), lambda e, s: (e, 0)),
        ],
        out_specs=[pl.BlockSpec((rows, n), lambda e, s: (0, 0))] * 2,
    )
    return pl.pallas_call(
        keys_kernel,
        grid_spec=grid_spec,
        out_shape=[jax.ShapeDtypeStruct((rows, n), got.dtype)] * 2,
        compiler_params=params(),
        name="keys",
    )(core, got, target, cosine, sine)


def attend_kernel(d, core, got, target, *refs):
    *blocks, cosine, sine, qdocs, kdocs, out, q, kv = refs
    rows = out.shape[0]
    heads = got.shape[-1] // HEAD
    span = rows + QT
    v = unpack_rows(got[...].reshape(-1, got.shape[-1]), target[0], rows)
    for h in range(heads):
        q[h] = rotated(v[:, h * HEAD : (h + 1) * HEAD], cosine[...], sine[...]).astype(q.dtype)
    for e in range(2):

        @pl.when(d ^ core[0] == e)
        def _(e=e):
            kv[:rows] = blocks[e][...]
            kv[rows:] = blocks[e + 1][...]

    scale = HEAD**-0.5

    def tile(i, carry):
        at = pl.multiple_of(i * QT, QT)
        qs = q[:, pl.ds(at, QT), :].reshape(heads * QT, HEAD)
        ks = kv[pl.ds(at, span), :HEAD]
        vs = kv[pl.ds(at, span), HEAD:]
        s = lax.dot_general(
            qs, ks, (((1,), (1,)), ((), ())), preferred_element_type=jnp.float32
        ).reshape(heads, QT, span)
        behind = lax.broadcasted_iota(jnp.int32, (QT, span), 1) - lax.broadcasted_iota(
            jnp.int32, (QT, span), 0
        )
        ok = (behind > 0) & (behind <= rows) & (
            qdocs[pl.ds(at, QT), :1] == kdocs[0, :, pl.ds(at, span)]
        )
        s = jnp.where(ok[None], s * scale, MASKED)
        top = jnp.max(s, axis=-1, keepdims=True)
        w = jnp.exp(s - top)
        total = jnp.sum(w, axis=-1, keepdims=True)
        o = jnp.dot(
            w.astype(kv.dtype).reshape(heads * QT, span), vs, preferred_element_type=jnp.float32
        ).reshape(heads, QT, HEAD)
        o = o / total
        for h in range(heads):
            out[pl.ds(at, QT), h * HEAD : (h + 1) * HEAD] = o[h].astype(out.dtype)
        return carry

    lax.fori_loop(0, rows // QT, tile, 0)


def attend(d, core, got, target, kv3, cosine, sine, qdocs, kdocs, rows):
    chips, _, _, cap, n = got.shape
    grid_spec = pltpu.PrefetchScalarGridSpec(
        num_scalar_prefetch=1,
        grid=(1,),
        in_specs=[
            pl.BlockSpec((chips, 2, 1, cap, n), lambda i, s: (0, 0, d, 0, 0)),
            pl.BlockSpec((1, 1, chips * 2 * cap), lambda i, s: (d, 0, 0)),
            *[pl.BlockSpec((rows, 2 * HEAD), lambda i, s: (0, 0))] * 3,
            pl.BlockSpec((rows, HEAD), lambda i, s: (d ^ s[0], 0)),
            pl.BlockSpec((rows, HEAD), lambda i, s: (d ^ s[0], 0)),
            pl.BlockSpec((rows, HEAD), lambda i, s: (d ^ s[0], 0)),
            pl.BlockSpec((1, 1, 2 * rows), lambda i, s: (d ^ s[0], 0, 0)),
        ],
        out_specs=pl.BlockSpec((rows, n), lambda i, s: (0, 0)),
        scratch_shapes=[
            pltpu.VMEM((n // HEAD, rows, HEAD), got.dtype),
            pltpu.VMEM((2 * rows, 2 * HEAD), got.dtype),
        ],
    )
    return pl.pallas_call(
        functools.partial(attend_kernel, d),
        grid_spec=grid_spec,
        out_shape=jax.ShapeDtypeStruct((rows, n), got.dtype),
        compiler_params=params(),
        name="attend",
    )(core, got, target, *kv3, cosine, sine, qdocs, kdocs)


def join_kernel(place, a, b, c, d, out):
    i = pl.program_id(0)
    for k, piece in enumerate((a, b, c, d)):

        @pl.when(i == k)
        def _(piece=piece):
            out[...] = piece[...]


def join(part, pieces):
    rows, n = pieces[0].shape
    grid_spec = pltpu.PrefetchScalarGridSpec(
        num_scalar_prefetch=1,
        grid=(len(pieces),),
        in_specs=[pl.BlockSpec((rows, n), lambda i, s: (0, 0)) for _ in pieces],
        out_specs=pl.BlockSpec((rows, n), lambda i, s: (0, s[0] ^ i)),
    )
    return pl.pallas_call(
        join_kernel,
        grid_spec=grid_spec,
        out_shape=jax.ShapeDtypeStruct((rows, n * len(pieces)), pieces[0].dtype),
        compiler_params=params(),
        name="join",
    )(part, *pieces)


def chip_cycle(chips):
    return list(range(0, chips, 2)) + list(range(chips - 1 - chips % 2, 0, -2))


def ring_gather(shard, chips):
    order = chip_cycle(chips)

    def pairs(step):
        return [
            (2 * order[i] + c, 2 * order[(i + step) % chips] + c)
            for i in range(chips)
            for c in range(2)
        ]

    forth, back = pairs(1), pairs(-1)
    found = [shard]
    a = b = shard
    for hop in range(chips // 2):
        a = lax.ppermute(a, "ctx", forth)
        found.append(a)
        if hop < (chips - 1) // 2:
            b = lax.ppermute(b, "ctx", back)
            found.append(b)
    return found


def ring_sources(chip, chips):
    order = jnp.array(chip_cycle(chips), jnp.int32)
    place = jnp.sum(jnp.where(order == chip, jnp.arange(chips, dtype=jnp.int32), 0))
    steps = [0]
    for hop in range(chips // 2):
        steps.append(-(hop + 1))
        if hop < (chips - 1) // 2:
            steps.append(hop + 1)
    return order[(place + jnp.array(steps, jnp.int32)) % chips]


def layer(hidden, dest, doc_ids, w_query, key_weight, value_weight):
    rows = hidden.shape[0]
    dp = lax.axis_size("dp")
    size = lax.axis_size("ctx")
    chips = size // 2
    cap = 2 * rows // size
    index = lax.axis_index("ctx")
    chip = index // 2
    core = index % 2
    part = (lax.axis_index("dp") % 2) * 2 + core
    parts = 4
    kq = w_query.shape[1] // parts
    kk = key_weight.shape[1] // parts
    depth = w_query.shape[0]

    core_pairs = [(i, i ^ 1) for i in range(size)]
    side_pairs = [(i, i ^ 1) for i in range(dp)]
    same_core = [[2 * i + c for i in range(chips)] for c in range(2)]

    def to_core(x):
        return lax.ppermute(x, "ctx", core_pairs)

    def to_side(x):
        return lax.ppermute(x, "dp", side_pairs)

    def exchange(x):
        return lax.all_to_all(
            x, "ctx", split_axis=0, concat_axis=0, tiled=True, axis_index_groups=same_core
        )

    ints = to_side(jnp.concatenate([dest, doc_ids]))
    beside = to_side(hidden)

    def columns(g):
        return jnp.concatenate(
            [
                lax.dynamic_slice_in_dim(key_weight, g * kk, kk, 1),
                lax.dynamic_slice_in_dim(value_weight, g * kk, kk, 1),
                lax.dynamic_slice_in_dim(w_query, g * kq, kq, 1),
            ],
            axis=1,
        )

    shard = jnp.concatenate([columns(part), to_core(columns(part ^ 1))], axis=0)
    ws_kv = ring_gather(shard[:, : 2 * kk], chips)
    ws_q = ring_gather(shard[:, 2 * kk :], chips)
    sources = ring_sources(chip, chips)
    koff = (
        jnp.stack([2 * sources + core, 2 * sources + 1 - core], axis=1).reshape(-1) * depth
    ).astype(jnp.int32)

    across = to_core(hidden)
    diagonal = to_core(beside)
    xs = ((hidden, across), (beside, diagonal))

    both = jnp.stack([dest, ints[:rows]])
    tables = lax.all_to_all(
        jnp.broadcast_to(both[None], (size, 2, rows)),
        "ctx",
        split_axis=0,
        concat_axis=0,
        tiled=True,
    )
    tables = jnp.moveaxis(tables, 1, 0).reshape(2, chips, 2, rows)
    tables = jnp.where(core == 0, tables, tables[:, :, ::-1])
    block = tables // rows
    local = tables % rows
    before = (
        jnp.arange(rows, dtype=jnp.int32)[:, None] < jnp.arange(rows, dtype=jnp.int32)[None, :]
    ).astype(jnp.bfloat16)

    def rank_in(hit):
        return jnp.dot(
            hit.astype(jnp.bfloat16), before, preferred_element_type=jnp.float32
        ).astype(jnp.int32)

    leaving = lax.dynamic_index_in_dim(block, chip, 1, keepdims=False)
    hit = leaving[:, :, None, :] == jnp.arange(size, dtype=jnp.int32)[None, None, :, None]
    rank = jnp.sum(jnp.where(hit, rank_in(hit), 0), axis=2)
    slots = (leaving // 2) * (2 * cap) + ((leaving % 2) ^ core) * cap + rank
    slots = slots.reshape(2, 2, 1, rows)

    mine = 2 * chip + (jnp.arange(2, dtype=jnp.int32) ^ core)
    hit = block[:, None] == mine[None, :, None, None, None]
    rank = rank_in(hit)
    at_slot = hit[..., None, :] & (
        rank[..., None, :] == jnp.arange(cap, dtype=jnp.int32)[:, None]
    )
    targets = jnp.sum(jnp.where(at_slot, local[:, None, :, :, None, :] + 1, 0), axis=-1) - 1
    targets = targets.reshape(2, 2, 1, size * cap)

    half = HEAD // 2
    freq = jnp.arange(half, dtype=jnp.float32)
    inverse = jnp.exp(-(2.0 * freq / HEAD) * jnp.log(jnp.float32(ROPE_BASE)))
    positions = chip * 2 * rows + jnp.arange(2 * rows, dtype=jnp.int32)
    angles = positions.astype(jnp.float32)[:, None] * inverse[None, :]
    cos_half, sin_half = jnp.cos(angles), jnp.sin(angles)
    cosine = jnp.concatenate([cos_half, cos_half], axis=1)
    sine = jnp.concatenate([-sin_half, sin_half], axis=1)
    core_ref = core.reshape(1).astype(jnp.int32)

    def doc_tables(docs):
        padded = jnp.concatenate([jnp.full((rows,), -1, jnp.int32), docs])
        near = lax.dynamic_slice_in_dim(padded, chip * 2 * rows, 3 * rows, 0)
        qdocs = jnp.broadcast_to(near[rows:, None], (2 * rows, HEAD))
        kdocs = jnp.stack([near[: 2 * rows], near[rows:]])[:, None, :]
        return qdocs, kdocs

    docs = (doc_tables(doc_ids), doc_tables(ints[rows:]))
    ahead = [(i, i + 2) for i in range(size - 2)]

    def send(t, ws):
        out = project(*xs[t], slots[t], ws, koff, 2 * cap)
        got = exchange(out.reshape(chips, 4 * cap, out.shape[-1]))
        return got.reshape(chips, 2, 2, cap, out.shape[-1])

    def keys_of(t, got):
        first, second = unpack_keys(core_ref, got, targets[t], cosine, sine, rows)
        return lax.ppermute(second, "ctx", ahead), first, second

    def result(t, d, got, kv3):
        return attend(d, core_ref, got, targets[t], kv3, cosine, sine, *docs[t], rows)

    kv_own = keys_of(0, send(0, ws_kv))
    kv_side = keys_of(1, send(1, ws_kv))
    got_side = send(1, ws_q)
    got_own = send(0, ws_q)
    far = to_side(result(1, 1, got_side, kv_side))
    far = to_core(far)
    near = to_side(result(1, 0, got_side, kv_side))
    other = to_core(result(0, 1, got_own, kv_own))
    own = result(0, 0, got_own, kv_own)
    return join(part.reshape(1).astype(jnp.int32), (own, other, near, far))


def solution(mesh):
    placed = (
        P(("dp", "ctx"), None),
        P(("dp", "ctx")),
        P("dp"),
        P("ctx", None),
        P("ctx", None),
        P("ctx", None),
    )
    return jax.shard_map(
        layer, mesh=mesh, in_specs=placed, out_specs=P(("dp", "ctx"), None), check_vma=False
    )
```

profile of v0, /device:TPU:16, one launch (start us, length us, event | category | flops | bytes accessed | tf_op | source)
XLA Modules:
  0.0 422.7 jit_solution(7954875927677895491)
XLA Ops:
  0.0 1.6 collective-permute-start.19
  2.6 90.1 %collective-permute-done.19.x0 = bf16[512,4096]{1,0:T(8,128)(2,1)} collective-permute-done((bf16[512,4096]{1,0:T(8,128)(2,1)}, bf16[512,4096]{1,0:T(8,128)(2,1)}, u32[]{:S(2)}, u32[]{:S(2)}) %collective-permute-start.19) | collective-permute-done | bytes 4194336 | tf_op jit(solution)/shard_map/ppermute | solution.py:296
  94.3 1.6 collective-permute-start.1
  96.5 4.1 collective-permute-done.2
  100.7 1.6 collective-permute-start.10
  104.3 5.2 %all-to-all-start = ((s32[16,2,512]{2,1,0:T(2,128)}), s32[16,2,512]{2,1,0:T(2,128)S(1)}, u32[]{:S(2)}, u32[]{:S(2)}) async-start(s32[16,2,512]{2,1,0:T(2,128)} %broadcast_in_dim.34), calls=%async_computation | async-start | bytes 131072 | tf_op jit(solution)/shard_map/all_to_all | solution.py:329
  110.1 1.5 collective-permute-start.12
  112.3 1.5 all-to-all-done
  113.8 5.0 %collective-permute-done.11.refs_2_ = bf16[512,256]{1,0:T(8,128)(2,1)S(1)} collective-permute-done((bf16[512,256]{1,0:T(8,128)(2,1)S(1)}, bf16[512,256]{1,0:T(8,128)(2,1)S(1)}, u32[]{:S(2)}, u32[]{:S(2)}) %collective-permute-start.11) | collective-permute-done | bytes 262176 | tf_op jit(solution)/shard_map/ppermute | solution.py:257
  121.2 5.4 %collective-permute-done.13.refs_4_ = bf16[512,256]{1,0:T(8,128)(2,1)S(1)} collective-permute-done((bf16[512,256]{1,0:T(8,128)(2,1)S(1)}, bf16[512,256]{1,0:T(8,128)(2,1)S(1)}, u32[]{:S(2)}, u32[]{:S(2)}) %collective-permute-start.13) | collective-permute-done | bytes 262176 | tf_op jit(solution)/shard_map/ppermute | solution.py:257
  129.3 4.2 collective-permute-done.15.refs_6_
  134.9 9.2 %project.5 = bf16[8,2,128,256]{3,2,1,0:T(8,128)(2,1)} custom-call(s32[16]{0:T(128)} %mul.90.koff, bf16[512,4096]{1,0:T(8,128)(2,1)} %x0.3, bf16[512,4096]{1,0:T(8,128)(2,1)} %collective-permute-done.x1, s32[2,1,512]{2,1,0:T(1,128)} %get-tuple-element.28.slots, bf16[512,256]{1,0:T(8,128)(2,1)} %copy-done.5, bf16[512,256]{1,0:T(8,128)(2,1)} %copy-done.13, ...), custom_call_target="tpu_custom_call" | custom-call | tf_op jit(solution)/shard_map/project/pallas_call | solution.py:82
  144.1 5.8 %all-to-all-start.2 = ((bf16[8,256,256]{2,1,0:T(8,128)(2,1)}), bf16[8,256,256]{2,1,0:T(8,128)(2,1)S(1)}, u32[]{:S(2)}, u32[]{:S(2)}) async-start(bf16[8,256,256]{2,1,0:T(8,128)(2,1)} %bitcast.62), calls=%async_computation.2 | async-start | bytes 2097152 | tf_op jit(solution)/shard_map/all_to_all | solution.py:299
  149.9 1.5 collective-permute-start.3
  151.5 9.2 %project.7 = bf16[8,2,128,256]{3,2,1,0:T(8,128)(2,1)} custom-call(s32[16]{0:T(128)} %mul.90.koff, bf16[512,4096]{1,0:T(8,128)(2,1)} %collective-permute-done.19.x0, bf16[512,4096]{1,0:T(8,128)(2,1)} %collective-permute-done.20.x1, s32[2,1,512]{2,1,0:T(1,128)} %get-tuple-element.27.slots, bf16[512,256]{1,0:T(8,128)(2,1)} %copy-done.5, ...), custom_call_target="tpu_custom_call" | custom-call | tf_op jit(solution)/shard_map/project/pallas_call | solution.py:82
  160.7 9.8 %all-to-all-done.2 = bf16[8,256,256]{2,1,0:T(8,128)(2,1)S(1)} async-done(((bf16[8,256,256]{2,1,0:T(8,128)(2,1)}), bf16[8,256,256]{2,1,0:T(8,128)(2,1)S(1)}, u32[]{:S(2)}, u32[]{:S(2)}) %all-to-all-start.2) | async-done | bytes 1048608 | tf_op jit(solution)/shard_map/all_to_all | solution.py:299
  170.5 7.8 %all-to-all-start.4 = ((bf16[8,256,256]{2,1,0:T(8,128)(2,1)}), bf16[8,256,256]{2,1,0:T(8,128)(2,1)S(1)}, u32[]{:S(2)}, u32[]{:S(2)}) async-start(bf16[8,256,256]{2,1,0:T(8,128)(2,1)} %bitcast.61), calls=%async_computation.4 | async-start | bytes 2097152 | tf_op jit(solution)/shard_map/all_to_all | solution.py:299
  178.9 14.7 %collective-permute-done.3.refs_1_ = bf16[512,512]{1,0:T(8,128)(2,1)S(1)} collective-permute-done((bf16[512,512]{1,0:T(8,128)(2,1)S(1)}, bf16[512,512]{1,0:T(8,128)(2,1)S(1)}, u32[]{:S(2)}, u32[]{:S(2)}) %collective-permute-start.3) | collective-permute-done | bytes 524320 | tf_op jit(solution)/shard_map/ppermute | solution.py:254
  193.5 17.1 %collective-permute-done.4.refs_2_ = bf16[512,512]{1,0:T(8,128)(2,1)S(1)} collective-permute-done((bf16[512,512]{1,0:T(8,128)(2,1)S(1)}, bf16[512,512]{1,0:T(8,128)(2,1)S(1)}, u32[]{:S(2)}, u32[]{:S(2)}) %collective-permute-start.4) | collective-permute-done | bytes 524320 | tf_op jit(solution)/shard_map/ppermute | solution.py:257
  210.7 2.5 collective-permute-start.6
  213.1 3.1 collective-permute-done.5.refs_3_
  216.2 6.5 %collective-permute-done.6.refs_4_ = bf16[512,512]{1,0:T(8,128)(2,1)S(1)} collective-permute-done((bf16[512,512]{1,0:T(8,128)(2,1)S(1)}, bf16[512,512]{1,0:T(8,128)(2,1)S(1)}, u32[]{:S(2)}, u32[]{:S(2)}) %collective-permute-start.6) | collective-permute-done | bytes 524320 | tf_op jit(solution)/shard_map/ppermute | solution.py:257
  222.8 2.5 collective-permute-start.8
  225.2 3.4 collective-permute-done.7.refs_5_
  228.9 4.7 %collective-permute-done.8.refs_6_ = bf16[512,512]{1,0:T(8,128)(2,1)S(1)} collective-permute-done((bf16[512,512]{1,0:T(8,128)(2,1)S(1)}, bf16[512,512]{1,0:T(8,128)(2,1)S(1)}, u32[]{:S(2)}, u32[]{:S(2)}) %collective-permute-start.8) | collective-permute-done | bytes 524320 | tf_op jit(solution)/shard_map/ppermute | solution.py:257
  233.6 6.6 %collective-permute-done.9.refs_7_ = bf16[512,512]{1,0:T(8,128)(2,1)S(1)} collective-permute-done((bf16[512,512]{1,0:T(8,128)(2,1)S(1)}, bf16[512,512]{1,0:T(8,128)(2,1)S(1)}, u32[]{:S(2)}, u32[]{:S(2)}) %collective-permute-start.9) | collective-permute-done | bytes 524320 | tf_op jit(solution)/shard_map/ppermute | solution.py:254
  241.0 12.4 %project.6 = bf16[8,2,128,512]{3,2,1,0:T(8,128)(2,1)} custom-call(s32[16]{0:T(128)} %mul.90.koff, bf16[512,4096]{1,0:T(8,128)(2,1)} %collective-permute-done.19.x0, bf16[512,4096]{1,0:T(8,128)(2,1)} %collective-permute-done.20.x1, s32[2,1,512]{2,1,0:T(1,128)} %get-tuple-element.27.slots, bf16[512,512]{1,0:T(8,128)(2,1)} %copy-done.2, ...), custom_call_target="tpu_custom_call" | custom-call | tf_op jit(solution)/shard_map/project/pallas_call | solution.py:82
  254.4 4.2 all-to-all-start.3
  258.6 12.4 %project.4 = bf16[8,2,128,512]{3,2,1,0:T(8,128)(2,1)} custom-call(s32[16]{0:T(128)} %mul.90.koff, bf16[512,4096]{1,0:T(8,128)(2,1)} %x0.3, bf16[512,4096]{1,0:T(8,128)(2,1)} %collective-permute-done.x1, s32[2,1,512]{2,1,0:T(1,128)} %get-tuple-element.28.slots, bf16[512,512]{1,0:T(8,128)(2,1)} %copy-done.2, bf16[512,512]{1,0:T(8,128)(2,1)} %copy-done.6, ...), custom_call_target="tpu_custom_call" | custom-call | tf_op jit(solution)/shard_map/project/pallas_call | solution.py:82
  271.0 31.2 %all-to-all-done.3 = bf16[8,256,512]{2,1,0:T(8,128)(2,1)S(1)} async-done(((bf16[8,256,512]{2,1,0:T(8,128)(2,1)}), bf16[8,256,512]{2,1,0:T(8,128)(2,1)S(1)}, u32[]{:S(2)}, u32[]{:S(2)}) %all-to-all-start.3) | async-done | bytes 2097184 | tf_op jit(solution)/shard_map/all_to_all | solution.py:299
  302.2 1.3 copy-done.1
  303.5 7.5 %all-to-all-start.1 = ((bf16[8,256,512]{2,1,0:T(8,128)(2,1)}), bf16[8,256,512]{2,1,0:T(8,128)(2,1)}, u32[]{:S(2)}, u32[]{:S(2)}) async-start(bf16[8,256,512]{2,1,0:T(8,128)(2,1)} %bitcast.57), calls=%async_computation.1 | async-start | bytes 4194304 | tf_op jit(solution)/shard_map/all_to_all | solution.py:299
  311.1 1.9 fusion.7
  313.0 1.3 pad_maximum_fusion.1
  314.9 1.9 select_reduce_fusion
  317.5 3.1 keys.3
  320.6 3.4 collective-permute-start.21
  324.7 38.3 %collective-permute-done.21.refs_0_ = bf16[512,256]{1,0:T(8,128)(2,1)S(1)} collective-permute-done((bf16[512,256]{1,0:T(8,128)(2,1)}, bf16[512,256]{1,0:T(8,128)(2,1)S(1)}, u32[]{:S(2)}, u32[]{:S(2)}) %collective-permute-start.21) | collective-permute-done | bytes 262176 | tf_op jit(solution)/shard_map/ppermute | solution.py:391
  364.0 7.5 %attend.7 = bf16[512,512]{1,0:T(8,128)(2,1)} custom-call(s32[1]{0:T(128)} %bitcast.1.core, bf16[8,2,2,64,512]{4,3,2,1,0:T(8,128)(2,1)} %bitcast.55, s32[2,1,1024]{2,1,0:T(1,128)} %squeeze.26.target, bf16[512,256]{1,0:T(8,128)(2,1)} %copy-done.16, bf16[512,256]{1,0:T(8,128)(2,1)} %get-tuple-element.12.refs_1_, bf16[512,256]{1,0:T(8,128)(2,1)} %get-tuple-element.11.refs_2_, ...), custom_call_target="tpu_custom_call" | custom-call | tf_op jit(solution)/shard_map/attend/pallas_call | solution.py:201
  371.4 1.5 collective-permute-start.23
  373.6 3.2 keys.2
  376.8 1.9 collective-permute-start.17
  379.4 8.3 %collective-permute-done.17.refs_0_ = bf16[512,256]{1,0:T(8,128)(2,1)S(1)} collective-permute-done((bf16[512,256]{1,0:T(8,128)(2,1)}, bf16[512,256]{1,0:T(8,128)(2,1)S(1)}, u32[]{:S(2)}, u32[]{:S(2)}) %collective-permute-start.17) | collective-permute-done | bytes 262176 | tf_op jit(solution)/shard_map/ppermute | solution.py:391
  388.7 7.4 %attend.5 = bf16[512,512]{1,0:T(8,128)(2,1)} custom-call(s32[1]{0:T(128)} %bitcast.1.core, bf16[8,2,2,64,512]{4,3,2,1,0:T(8,128)(2,1)} %bitcast.15.got, s32[2,1,1024]{2,1,0:T(1,128)} %squeeze.24.target, bf16[512,256]{1,0:T(8,128)(2,1)} %copy-done.19, bf16[512,256]{1,0:T(8,128)(2,1)} %get-tuple-element.10.refs_1_, bf16[512,256]{1,0:T(8,128)(2,1)} %get-tuple-element.9.refs_2_, ...), custom_call_target="tpu_custom_call" | custom-call | tf_op jit(solution)/shard_map/attend/pallas_call | solution.py:201
  396.1 7.6 %attend.6 = bf16[512,512]{1,0:T(8,128)(2,1)} custom-call(s32[1]{0:T(128)} %bitcast.1.core, bf16[8,2,2,64,512]{4,3,2,1,0:T(8,128)(2,1)} %bitcast.56, s32[2,1,1024]{2,1,0:T(1,128)} %squeeze.26.target, bf16[512,256]{1,0:T(8,128)(2,1)} %copy-done.16, bf16[512,256]{1,0:T(8,128)(2,1)} %get-tuple-element.12.refs_1_, bf16[512,256]{1,0:T(8,128)(2,1)} %get-tuple-element.11.refs_2_, ...), custom_call_target="tpu_custom_call" | custom-call | tf_op jit(solution)/shard_map/attend/pallas_call | solution.py:201
  404.5 7.4 %attend.4.a = bf16[512,512]{1,0:T(8,128)(2,1)} custom-call(s32[1]{0:T(128)} %bitcast.1.core, bf16[8,2,2,64,512]{4,3,2,1,0:T(8,128)(2,1)} %bitcast.15.got, s32[2,1,1024]{2,1,0:T(1,128)} %squeeze.24.target, bf16[512,256]{1,0:T(8,128)(2,1)} %copy-done.19, bf16[512,256]{1,0:T(8,128)(2,1)} %get-tuple-element.10.refs_1_, ...), custom_call_target="tpu_custom_call" | custom-call | tf_op jit(solution)/shard_map/attend/pallas_call | solution.py:201
  411.9 6.4 %collective-permute-done.22.c = bf16[512,512]{1,0:T(8,128)(2,1)S(1)} collective-permute-done((bf16[512,512]{1,0:T(8,128)(2,1)}, bf16[512,512]{1,0:T(8,128)(2,1)S(1)}, u32[]{:S(2)}, u32[]{:S(2)}) %collective-permute-start.22) | collective-permute-done | bytes 524320 | tf_op jit(solution)/shard_map/ppermute | solution.py:296
  419.3 3.4 join.1
  (134 shorter events, 23.0 us)
Async XLA Ops:
  0.0 95.9 %copy-start = (s32[8]{0:T(128)S(1)}, s32[8]{0:T(128)}, u32[]{:S(2)}) copy-start(s32[8]{0:T(128)} %constant.131.clone) | copy-start | bytes 100
  0.0 102.3 %copy-start.30 = (s32[8]{0:T(128)S(1)}, s32[8]{0:T(128)}, u32[]{:S(2)}) copy-start(s32[8]{0:T(128)} %constant.132.clone) | copy-start | bytes 100
  0.0 94.3 %copy-start.25 = (s32[8192]{0:T(1024)S(1)}, s32[8192]{0:T(1024)}, u32[]{:S(2)}) copy-start(s32[8192]{0:T(1024)} %param.10) | copy-start | bytes 98308
  0.0 94.3 %copy-start.29 = (s32[512]{0:T(512)S(1)}, s32[512]{0:T(512)}, u32[]{:S(2)}) copy-start(s32[512]{0:T(512)} %param.9) | copy-start | bytes 6148
  0.0 92.7 %collective-permute-start.19 = (bf16[512,4096]{1,0:T(8,128)(2,1)}, bf16[512,4096]{1,0:T(8,128)(2,1)}, u32[]{:S(2)}, u32[]{:S(2)}) collective-permute-start(bf16[512,4096]{1,0:T(8,128)(2,1)} %x0.3), channel_id=1, source_target_pairs={{0,16},{16,0},{1,17},{17,1},{2,18},{18,2},{3,19},{19,3},{4,20},{20... | collective-permute-start | bytes 12582920 | tf_op jit(solution)/shard_map/ppermute | solution.py:296
  1.6 132.6 %collective-permute-start = (bf16[512,4096]{1,0:T(8,128)(2,1)}, bf16[512,4096]{1,0:T(8,128)(2,1)}, u32[]{:S(2)}, u32[]{:S(2)}) collective-permute-start(bf16[512,4096]{1,0:T(8,128)(2,1)} %x0.3), channel_id=1, source_target_pairs={{0,1},{1,0},{2,3},{3,2},{4,5},{5,4},{6,7},{7,6},{8,9},{9,8},{10,11... | collective-permute-start | bytes 12582920 | tf_op jit(solution)/shard_map/ppermute | solution.py:293
  92.7 58.7 %collective-permute-start.20 = (bf16[512,4096]{1,0:T(8,128)(2,1)}, bf16[512,4096]{1,0:T(8,128)(2,1)}, u32[]{:S(2)}, u32[]{:S(2)}) collective-permute-start(bf16[512,4096]{1,0:T(8,128)(2,1)} %collective-permute-done.19.x0), channel_id=1, source_target_pairs={{0,1},{1,0},{2,3},{3,2},{4,5},{5,4},{6,7},{7,6},{8,9},{9,8},{10,11... | collective-permute-start | bytes 12582920 | tf_op jit(solution)/shard_map/ppermute | solution.py:293
  93.7 6.9 %collective-permute-start.2 = (bf16[256,768]{1,0:T(8,128)(2,1)S(1)}, bf16[256,768]{1,0:T(8,128)(2,1)S(1)}, u32[]{:S(2)}, u32[]{:S(2)}) collective-permute-start(bf16[256,768]{1,0:T(8,128)(2,1)S(1)} %pad_maximum_fusion.3), channel_id=1, source_target_pairs={{0,1},{1,0},{2,3},{3,2},{4,5},{5,4},{6,7},{7,6},{8,9},{9,8},{10,11... | collective-permute-start | bytes 1179656 | tf_op jit(solution)/shard_map/ppermute | solution.py:293
  94.3 9.3 %collective-permute-start.1 = (s32[8704]{0:T(1024)S(1)}, s32[8704]{0:T(1024)S(1)}, u32[]{:S(2)}, u32[]{:S(2)}) collective-permute-start(s32[8704]{0:T(1024)S(1)} %pad_add_fusion), channel_id=1, source_target_pairs={{0,16},{16,0},{1,17},{17,1},{2,18},{18,2},{3,19},{19,3},{4,20},{20... | collective-permute-start | bytes 104456 | tf_op jit(solution)/shard_map/ppermute | solution.py:296
  100.7 33.5 %copy-start.5 = (bf16[512,256]{1,0:T(8,128)(2,1)}, bf16[512,256]{1,0:T(8,128)(2,1)S(1)}, u32[]{:S(2)}) copy-start(bf16[512,256]{1,0:T(8,128)(2,1)S(1)} %pad_maximum_fusion.4.refs_0_) | copy-start | bytes 786436
  100.7 9.4 %collective-permute-start.10 = (bf16[512,256]{1,0:T(8,128)(2,1)S(1)}, bf16[512,256]{1,0:T(8,128)(2,1)S(1)}, u32[]{:S(2)}, u32[]{:S(2)}) collective-permute-start(bf16[512,256]{1,0:T(8,128)(2,1)S(1)} %pad_maximum_fusion.4.refs_0_), channel_id=1, source_target_pairs={{0,4},{1,5},{4,8},{5,9},{8,12},{9,13},{12,14},{13,15},{14,10},{15,... | collective-permute-start | bytes 786440 | tf_op jit(solution)/shard_map/ppermute | solution.py:254
  103.6 23.8 %copy-start.27 = (s32[8704]{0:T(1024)}, s32[8704]{0:T(1024)S(1)}, u32[]{:S(2)}) copy-start(s32[8704]{0:T(1024)S(1)} %collective-permute-done.1) | copy-start | bytes 104452
  104.3 9.5 %all-to-all-start = ((s32[16,2,512]{2,1,0:T(2,128)}), s32[16,2,512]{2,1,0:T(2,128)S(1)}, u32[]{:S(2)}, u32[]{:S(2)}) async-start(s32[16,2,512]{2,1,0:T(2,128)} %broadcast_in_dim.34), calls=%async_computation | async-start | bytes 131072 | tf_op jit(solution)/shard_map/all_to_all | solution.py:329
  109.5 9.3 %collective-permute-start.11 = (bf16[512,256]{1,0:T(8,128)(2,1)S(1)}, bf16[512,256]{1,0:T(8,128)(2,1)S(1)}, u32[]{:S(2)}, u32[]{:S(2)}) collective-permute-start(bf16[512,256]{1,0:T(8,128)(2,1)S(1)} %pad_maximum_fusion.4.refs_0_), channel_id=1, source_target_pairs={{0,2},{1,3},{4,0},{5,1},{8,4},{9,5},{12,8},{13,9},{14,12},{15,13},... | collective-permute-start | bytes 786440 | tf_op jit(solution)/shard_map/ppermute | solution.py:257
  110.1 24.1 %copy-start.13 = (bf16[512,256]{1,0:T(8,128)(2,1)}, bf16[512,256]{1,0:T(8,128)(2,1)S(1)}, u32[]{:S(2)}) copy-start(bf16[512,256]{1,0:T(8,128)(2,1)S(1)} %collective-permute-done.10.refs_1_) | copy-start | bytes 786436
  110.1 9.7 %collective-permute-start.12 = (bf16[512,256]{1,0:T(8,128)(2,1)S(1)}, bf16[512,256]{1,0:T(8,128)(2,1)S(1)}, u32[]{:S(2)}, u32[]{:S(2)}) collective-permute-start(bf16[512,256]{1,0:T(8,128)(2,1)S(1)} %collective-permute-done.10.refs_1_), channel_id=1, source_target_pairs={{0,4},{1,5},{4,8},{5,9},{8,12},{9,13},{12,14},{13,15},{14,10},{15,... | collective-permute-start | bytes 786440 | tf_op jit(solution)/shard_map/ppermute | solution.py:254
  118.8 15.4 %copy-start.14 = (bf16[512,256]{1,0:T(8,128)(2,1)}, bf16[512,256]{1,0:T(8,128)(2,1)S(1)}, u32[]{:S(2)}) copy-start(bf16[512,256]{1,0:T(8,128)(2,1)S(1)} %collective-permute-done.11.refs_2_) | copy-start | bytes 786436
  118.8 7.8 %collective-permute-start.13 = (bf16[512,256]{1,0:T(8,128)(2,1)S(1)}, bf16[512,256]{1,0:T(8,128)(2,1)S(1)}, u32[]{:S(2)}, u32[]{:S(2)}) collective-permute-start(bf16[512,256]{1,0:T(8,128)(2,1)S(1)} %collective-permute-done.11.refs_2_), channel_id=1, source_target_pairs={{0,2},{1,3},{4,0},{5,1},{8,4},{9,5},{12,8},{13,9},{14,12},{15,13},... | collective-permute-start | bytes 786440 | tf_op jit(solution)/shard_map/ppermute | solution.py:257
  119.7 14.5 %copy-start.15 = (bf16[512,256]{1,0:T(8,128)(2,1)}, bf16[512,256]{1,0:T(8,128)(2,1)S(1)}, u32[]{:S(2)}) copy-start(bf16[512,256]{1,0:T(8,128)(2,1)S(1)} %collective-permute-done.12.refs_3_) | copy-start | bytes 786436
  119.7 7.8 %collective-permute-start.14 = (bf16[512,256]{1,0:T(8,128)(2,1)S(1)}, bf16[512,256]{1,0:T(8,128)(2,1)S(1)}, u32[]{:S(2)}, u32[]{:S(2)}) collective-permute-start(bf16[512,256]{1,0:T(8,128)(2,1)S(1)} %collective-permute-done.12.refs_3_), channel_id=1, source_target_pairs={{0,4},{1,5},{4,8},{5,9},{8,12},{9,13},{12,14},{13,15},{14,10},{15,... | collective-permute-start | bytes 786440 | tf_op jit(solution)/shard_map/ppermute | solution.py:254
  126.5 7.6 %copy-start.17 = (bf16[512,256]{1,0:T(8,128)(2,1)}, bf16[512,256]{1,0:T(8,128)(2,1)S(1)}, u32[]{:S(2)}) copy-start(bf16[512,256]{1,0:T(8,128)(2,1)S(1)} %collective-permute-done.13.refs_4_) | copy-start | bytes 786436
  126.6 6.9 %collective-permute-start.15 = (bf16[512,256]{1,0:T(8,128)(2,1)S(1)}, bf16[512,256]{1,0:T(8,128)(2,1)S(1)}, u32[]{:S(2)}, u32[]{:S(2)}) collective-permute-start(bf16[512,256]{1,0:T(8,128)(2,1)S(1)} %collective-permute-done.13.refs_4_), channel_id=1, source_target_pairs={{0,2},{1,3},{4,0},{5,1},{8,4},{9,5},{12,8},{13,9},{14,12},{15,13},... | collective-permute-start | bytes 786440 | tf_op jit(solution)/shard_map/ppermute | solution.py:257
  127.5 6.7 %collective-permute-start.16 = (bf16[512,256]{1,0:T(8,128)(2,1)S(1)}, bf16[512,256]{1,0:T(8,128)(2,1)S(1)}, u32[]{:S(2)}, u32[]{:S(2)}) collective-permute-start(bf16[512,256]{1,0:T(8,128)(2,1)S(1)} %collective-permute-done.14.refs_5_), channel_id=1, source_target_pairs={{0,4},{1,5},{4,8},{5,9},{8,12},{9,13},{12,14},{13,15},{14,10},{15,... | collective-permute-start | bytes 786440 | tf_op jit(solution)/shard_map/ppermute | solution.py:254
  144.1 26.4 %all-to-all-start.2 = ((bf16[8,256,256]{2,1,0:T(8,128)(2,1)}), bf16[8,256,256]{2,1,0:T(8,128)(2,1)S(1)}, u32[]{:S(2)}, u32[]{:S(2)}) async-start(bf16[8,256,256]{2,1,0:T(8,128)(2,1)} %bitcast.62), calls=%async_computation.2 | async-start | bytes 2097152 | tf_op jit(solution)/shard_map/all_to_all | solution.py:299
  149.9 28.4 %copy-start.2 = (bf16[512,512]{1,0:T(8,128)(2,1)}, bf16[512,512]{1,0:T(8,128)(2,1)S(1)}, u32[]{:S(2)}) copy-start(bf16[512,512]{1,0:T(8,128)(2,1)S(1)} %slice.64.refs_0_) | copy-start | bytes 1572868
  149.9 43.6 %collective-permute-start.3 = (bf16[512,512]{1,0:T(8,128)(2,1)S(1)}, bf16[512,512]{1,0:T(8,128)(2,1)S(1)}, u32[]{:S(2)}, u32[]{:S(2)}) collective-permute-start(bf16[512,512]{1,0:T(8,128)(2,1)S(1)} %slice.64.refs_0_), channel_id=1, source_target_pairs={{0,4},{1,5},{4,8},{5,9},{8,12},{9,13},{12,14},{13,15},{14,10},{15,... | collective-permute-start | bytes 1572872 | tf_op jit(solution)/shard_map/ppermute | solution.py:254
  170.5 82.9 %copy-start.3 = (bf16[8,256,256]{2,1,0:T(8,128)(2,1)}, bf16[8,256,256]{2,1,0:T(8,128)(2,1)S(1)}, u32[]{:S(2)}) copy-start(bf16[8,256,256]{2,1,0:T(8,128)(2,1)S(1)} %all-to-all-done.2) | copy-start | bytes 3145732
  170.5 82.9 %all-to-all-start.4 = ((bf16[8,256,256]{2,1,0:T(8,128)(2,1)}), bf16[8,256,256]{2,1,0:T(8,128)(2,1)S(1)}, u32[]{:S(2)}, u32[]{:S(2)}) async-start(bf16[8,256,256]{2,1,0:T(8,128)(2,1)} %bitcast.61), calls=%async_computation.4 | async-start | bytes 2097152 | tf_op jit(solution)/shard_map/all_to_all | solution.py:299
  178.3 32.4 %collective-permute-start.4 = (bf16[512,512]{1,0:T(8,128)(2,1)S(1)}, bf16[512,512]{1,0:T(8,128)(2,1)S(1)}, u32[]{:S(2)}, u32[]{:S(2)}) collective-permute-start(bf16[512,512]{1,0:T(8,128)(2,1)S(1)} %slice.64.refs_0_), channel_id=1, source_target_pairs={{0,2},{1,3},{4,0},{5,1},{8,4},{9,5},{12,8},{13,9},{14,12},{15,13},... | collective-permute-start | bytes 1572872 | tf_op jit(solution)/shard_map/ppermute | solution.py:257
  193.5 46.6 %copy-start.6 = (bf16[512,512]{1,0:T(8,128)(2,1)}, bf16[512,512]{1,0:T(8,128)(2,1)S(1)}, u32[]{:S(2)}) copy-start(bf16[512,512]{1,0:T(8,128)(2,1)S(1)} %collective-permute-done.3.refs_1_) | copy-start | bytes 1572868
  193.5 22.7 %collective-permute-start.5 = (bf16[512,512]{1,0:T(8,128)(2,1)S(1)}, bf16[512,512]{1,0:T(8,128)(2,1)S(1)}, u32[]{:S(2)}, u32[]{:S(2)}) collective-permute-start(bf16[512,512]{1,0:T(8,128)(2,1)S(1)} %collective-permute-done.3.refs_1_), channel_id=1, source_target_pairs={{0,4},{1,5},{4,8},{5,9},{8,12},{9,13},{12,14},{13,15},{14,10},{15,... | collective-permute-start | bytes 1572872 | tf_op jit(solution)/shard_map/ppermute | solution.py:254
  210.7 29.5 %copy-start.7 = (bf16[512,512]{1,0:T(8,128)(2,1)}, bf16[512,512]{1,0:T(8,128)(2,1)S(1)}, u32[]{:S(2)}) copy-start(bf16[512,512]{1,0:T(8,128)(2,1)S(1)} %collective-permute-done.4.refs_2_) | copy-start | bytes 1572868
  210.7 12.1 %collective-permute-start.6 = (bf16[512,512]{1,0:T(8,128)(2,1)S(1)}, bf16[512,512]{1,0:T(8,128)(2,1)S(1)}, u32[]{:S(2)}, u32[]{:S(2)}) collective-permute-start(bf16[512,512]{1,0:T(8,128)(2,1)S(1)} %collective-permute-done.4.refs_2_), channel_id=1, source_target_pairs={{0,2},{1,3},{4,0},{5,1},{8,4},{9,5},{12,8},{13,9},{14,12},{15,13},... | collective-permute-start | bytes 1572872 | tf_op jit(solution)/shard_map/ppermute | solution.py:257
  216.2 23.9 %copy-start.8 = (bf16[512,512]{1,0:T(8,128)(2,1)}, bf16[512,512]{1,0:T(8,128)(2,1)S(1)}, u32[]{:S(2)}) copy-start(bf16[512,512]{1,0:T(8,128)(2,1)S(1)} %collective-permute-done.5.refs_3_) | copy-start | bytes 1572868
  216.2 12.4 %collective-permute-start.7 = (bf16[512,512]{1,0:T(8,128)(2,1)S(1)}, bf16[512,512]{1,0:T(8,128)(2,1)S(1)}, u32[]{:S(2)}, u32[]{:S(2)}) collective-permute-start(bf16[512,512]{1,0:T(8,128)(2,1)S(1)} %collective-permute-done.5.refs_3_), channel_id=1, source_target_pairs={{0,4},{1,5},{4,8},{5,9},{8,12},{9,13},{12,14},{13,15},{14,10},{15,... | collective-permute-start | bytes 1572872 | tf_op jit(solution)/shard_map/ppermute | solution.py:254
  222.7 17.4 %copy-start.9 = (bf16[512,512]{1,0:T(8,128)(2,1)}, bf16[512,512]{1,0:T(8,128)(2,1)S(1)}, u32[]{:S(2)}) copy-start(bf16[512,512]{1,0:T(8,128)(2,1)S(1)} %collective-permute-done.6.refs_4_) | copy-start | bytes 1572868
  222.8 10.9 %collective-permute-start.8 = (bf16[512,512]{1,0:T(8,128)(2,1)S(1)}, bf16[512,512]{1,0:T(8,128)(2,1)S(1)}, u32[]{:S(2)}, u32[]{:S(2)}) collective-permute-start(bf16[512,512]{1,0:T(8,128)(2,1)S(1)} %collective-permute-done.6.refs_4_), channel_id=1, source_target_pairs={{0,2},{1,3},{4,0},{5,1},{8,4},{9,5},{12,8},{13,9},{14,12},{15,13},... | collective-permute-start | bytes 1572872 | tf_op jit(solution)/shard_map/ppermute | solution.py:257
  228.6 11.6 %copy-start.10 = (bf16[512,512]{1,0:T(8,128)(2,1)}, bf16[512,512]{1,0:T(8,128)(2,1)S(1)}, u32[]{:S(2)}) copy-start(bf16[512,512]{1,0:T(8,128)(2,1)S(1)} %collective-permute-done.7.refs_5_) | copy-start | bytes 1572868
  228.6 11.5 %collective-permute-start.9 = (bf16[512,512]{1,0:T(8,128)(2,1)S(1)}, bf16[512,512]{1,0:T(8,128)(2,1)S(1)}, u32[]{:S(2)}, u32[]{:S(2)}) collective-permute-start(bf16[512,512]{1,0:T(8,128)(2,1)S(1)} %collective-permute-done.7.refs_5_), channel_id=1, source_target_pairs={{0,4},{1,5},{4,8},{5,9},{8,12},{9,13},{12,14},{13,15},{14,10},{15,... | collective-permute-start | bytes 1572872 | tf_op jit(solution)/shard_map/ppermute | solution.py:254
  254.4 47.8 %all-to-all-start.3 = ((bf16[8,256,512]{2,1,0:T(8,128)(2,1)}), bf16[8,256,512]{2,1,0:T(8,128)(2,1)S(1)}, u32[]{:S(2)}, u32[]{:S(2)}) async-start(bf16[8,256,512]{2,1,0:T(8,128)(2,1)} %bitcast.58), calls=%async_computation.3 | async-start | bytes 4194304 | tf_op jit(solution)/shard_map/all_to_all | solution.py:299
  303.5 84.2 %all-to-all-start.1 = ((bf16[8,256,512]{2,1,0:T(8,128)(2,1)}), bf16[8,256,512]{2,1,0:T(8,128)(2,1)}, u32[]{:S(2)}, u32[]{:S(2)}) async-start(bf16[8,256,512]{2,1,0:T(8,128)(2,1)} %bitcast.57), calls=%async_computation.1 | async-start | bytes 4194304 | tf_op jit(solution)/shard_map/all_to_all | solution.py:299
  314.3 9.7 %copy-start.28 = (s32[8704]{0:T(1024)S(1)}, s32[8704]{0:T(1024)}, u32[]{:S(2)}) copy-start(s32[8704]{0:T(1024)} %copy-done.27) | copy-start | bytes 104452
  320.6 42.4 %collective-permute-start.21 = (bf16[512,256]{1,0:T(8,128)(2,1)}, bf16[512,256]{1,0:T(8,128)(2,1)S(1)}, u32[]{:S(2)}, u32[]{:S(2)}) collective-permute-start(bf16[512,256]{1,0:T(8,128)(2,1)} %get-tuple-element.11.refs_2_), channel_id=1, source_target_pairs={{0,2},{1,3},{2,4},{3,5},{4,6},{5,7},{6,8},{7,9},{8,10},{9,11},{10,... | collective-permute-start | bytes 786440 | tf_op jit(solution)/shard_map/ppermute | solution.py:391
  371.4 32.8 %collective-permute-start.23 = (bf16[512,512]{1,0:T(8,128)(2,1)}, bf16[512,512]{1,0:T(8,128)(2,1)S(1)}, u32[]{:S(2)}, u32[]{:S(2)}) collective-permute-start(bf16[512,512]{1,0:T(8,128)(2,1)} %attend.7), channel_id=1, source_target_pairs={{0,16},{16,0},{1,17},{17,1},{2,18},{18,2},{3,19},{19,3},{4,20},{20... | collective-permute-start | bytes 1572872 | tf_op jit(solution)/shard_map/ppermute | solution.py:296
  376.8 10.9 %collective-permute-start.17 = (bf16[512,256]{1,0:T(8,128)(2,1)}, bf16[512,256]{1,0:T(8,128)(2,1)S(1)}, u32[]{:S(2)}, u32[]{:S(2)}) collective-permute-start(bf16[512,256]{1,0:T(8,128)(2,1)} %get-tuple-element.9.refs_2_), channel_id=1, source_target_pairs={{0,2},{1,3},{2,4},{3,5},{4,6},{5,7},{6,8},{7,9},{8,10},{9,11},{10,... | collective-permute-start | bytes 786440 | tf_op jit(solution)/shard_map/ppermute | solution.py:391
  396.1 15.8 %collective-permute-start.18 = (bf16[512,512]{1,0:T(8,128)(2,1)}, bf16[512,512]{1,0:T(8,128)(2,1)S(1)}, u32[]{:S(2)}, u32[]{:S(2)}) collective-permute-start(bf16[512,512]{1,0:T(8,128)(2,1)} %attend.5), channel_id=1, source_target_pairs={{0,1},{1,0},{2,3},{3,2},{4,5},{5,4},{6,7},{7,6},{8,9},{9,8},{10,11... | collective-permute-start | bytes 1572872 | tf_op jit(solution)/shard_map/ppermute | solution.py:293
  403.7 14.6 %collective-permute-start.22 = (bf16[512,512]{1,0:T(8,128)(2,1)}, bf16[512,512]{1,0:T(8,128)(2,1)S(1)}, u32[]{:S(2)}, u32[]{:S(2)}) collective-permute-start(bf16[512,512]{1,0:T(8,128)(2,1)} %attend.6), channel_id=1, source_target_pairs={{0,16},{16,0},{1,17},{17,1},{2,18},{18,2},{3,19},{19,3},{4,20},{20... | collective-permute-start | bytes 1572872 | tf_op jit(solution)/shard_map/ppermute | solution.py:296
  404.3 14.0 %collective-permute-start.24 = (bf16[512,512]{1,0:T(8,128)(2,1)S(1)}, bf16[512,512]{1,0:T(8,128)(2,1)S(1)}, u32[]{:S(2)}, u32[]{:S(2)}) collective-permute-start(bf16[512,512]{1,0:T(8,128)(2,1)S(1)} %collective-permute-done.23), channel_id=1, source_target_pairs={{0,1},{1,0},{2,3},{3,2},{4,5},{5,4},{6,7},{7,6},{8,9},{9,8},{10,11... | collective-permute-start | bytes 1572872 | tf_op jit(solution)/shard_map/ppermute | solution.py:293
  (13 other events, 35.3 us)
where the time goes:
time: 424 us; the launch traced here: 423 us
  waiting for transfers between devices  261 us (62%)
  Pallas kernels  82.8 us (20%)
  starting transfers between devices  56.7 us (13%)
  local copies, waits for them, and re-layouts  14.6 us (3%)
  other arithmetic  6.85 us (2%)
    ppermute x4, waiting for transfers between devices, to_side(): return lax.ppermute(x, 'dp', side_pairs)  96.4 us
    ppermute x2, waiting for transfers between devices, keys_of(): return (lax.ppermute(second, 'ctx', ahead), first, second)  46.6 us
    pallas_call x4, Pallas kernels, project(): pl.pallas_call(project_kernel, grid_spec=grid_spec, out_shape=jax.ShapeDt...  43.2 us
    ppermute x6, waiting for transfers between devices, ring_gather(): b = lax.ppermute(b, 'ctx', back)  42.9 us
    all_to_all x4, waiting for transfers between devices, exchange(): lax.all_to_all(x, 'ctx', split_axis=0, concat_axis=0, tiled=True, axis_in...  41 us
    pallas_call x4, Pallas kernels, attend(): pl.pallas_call(functools.partial(attend_kernel, d), grid_spec=grid_spec,...  29.9 us
    ppermute x8, waiting for transfers between devices, ring_gather(): a = lax.ppermute(a, 'ctx', forth)  28.4 us
    all_to_all x4, starting transfers between devices, exchange(): lax.all_to_all(x, 'ctx', split_axis=0, concat_axis=0, tiled=True, axis_in...  25.3 us
  transfers between devices with their start and end apart: 30, of which 19 were waited for; matrix products, arithmetic and copies ran while one was open for 4% of the time, Pallas kernels for 19%

commit v1 on v0

--- a/solution.py
+++ b/solution.py
@@ -12,6 +12,7 @@
 ROPE_BASE = 500000.0 * 16.0 ** (128.0 / 126.0)
 MASKED = -1e30
 QT = 128
+DP, CTX = "dp", "ctx"
 VMEM_LIMIT = 56 * 1024 * 1024
 
 
@@ -21,71 +22,60 @@
     )
 
 
-def project_kernel(koff, x0, x1, slots, *refs):
-    *ws, out, y = refs
+def project_kernel(koff, x, slots, *refs):
+    *refs, out, y = refs
     i = pl.program_id(0)
-    half = lax.rem(i, 2)
-    bm = x0.shape[0]
+    chips, _, per, n = out.shape
+    ws = refs[:chips]
+    rows = y.shape[0]
+    bm = x.shape[0]
     kk = ws[0].shape[0] // 2
-    n = ws[0].shape[1]
-
-    def compute(x):
-        acc = jnp.zeros((bm, n), jnp.float32)
-        for k, w in enumerate(ws):
-            for h in range(2):
-                off = pl.multiple_of(koff[2 * k + h], kk)
-                acc = acc + jnp.dot(
-                    x[:, pl.ds(off, kk)],
-                    w[h * kk : (h + 1) * kk, :],
-                    preferred_element_type=jnp.float32,
-                )
-        y[pl.ds(pl.multiple_of(half * bm, bm), bm), :] = acc.astype(y.dtype)
-
-    @pl.when(i < 2)
+    acc = jnp.zeros((bm, n), jnp.float32)
+    for k, w in enumerate(ws):
+        for h in range(2):
+            off = pl.multiple_of(koff[2 * k + h], kk)
+            acc = acc + jnp.dot(
+                x[:, pl.ds(off, kk)],
+                w[h * kk : (h + 1) * kk, :],
+                preferred_element_type=jnp.float32,
+            )
+    y[pl.ds(pl.multiple_of(i * bm, bm), bm), :] = acc.astype(y.dtype)
+
+    @pl.when(i == rows // bm - 1)
     def _():
-        compute(x0)
-
-    @pl.when(i >= 2)
-    def _():
-        compute(x1)
-
-    @pl.when(half == 1)
-    def _():
-        chips, _, per, _ = out.shape
-        rows = y.shape[0]
-        row_slot = slots[0]
         step = max(1, 256 // per)
         for a in range(0, chips, step):
             ids = lax.broadcasted_iota(jnp.int32, (step * per, rows), 0) + a * per
-            pick = jnp.where(ids == row_slot, 1.0, 0.0).astype(y.dtype)
+            pick = jnp.where(ids == slots[0], 1.0, 0.0).astype(y.dtype)
             part = jnp.dot(pick, y[...], preferred_element_type=jnp.float32)
             out[a : a + step, 0] = part.astype(out.dtype).reshape(step, per, n)
 
 
-def project(x0, x1, slots, ws, koff, per):
-    rows, width = x0.shape
+def project(x, slots, ws, koff, per, s, base=None):
+    rows, width = x.shape
     n = ws[0].shape[1]
     chips = len(ws)
     bm = rows // 2
+    more = [] if base is None else [base]
     grid_spec = pltpu.PrefetchScalarGridSpec(
         num_scalar_prefetch=1,
-        grid=(4,),
+        grid=(2,),
         in_specs=[
-            pl.BlockSpec((bm, width), lambda i, s: (jnp.minimum(i, 1), 0)),
-            pl.BlockSpec((bm, width), lambda i, s: (jnp.maximum(i - 2, 0), 0)),
-            pl.BlockSpec((1, 1, rows), lambda i, s: (i // 2, 0, 0)),
+            pl.BlockSpec((bm, width), lambda i, k: (i, 0)),
+            pl.BlockSpec((1, 1, rows), lambda i, k: (s, 0, 0)),
         ]
-        + [pl.BlockSpec(w.shape, lambda i, s: (0, 0)) for w in ws],
-        out_specs=pl.BlockSpec((chips, 1, per, n), lambda i, s: (0, i // 2, 0, 0)),
-        scratch_shapes=[pltpu.VMEM((rows, n), x0.dtype)],
+        + [pl.BlockSpec(w.shape, lambda i, k: (0, 0)) for w in ws]
+        + [pl.BlockSpec(memory_space=pl.ANY) for _ in more],
+        out_specs=pl.BlockSpec((chips, 1, per, n), lambda i, k: (0, s, 0, 0)),
+        scratch_shapes=[pltpu.VMEM((rows, n), x.dtype)],
     )
     return pl.pallas_call(
         project_kernel,
         grid_spec=grid_spec,
-        out_shape=jax.ShapeDtypeStruct((chips, 2, per, n), x0.dtype),
+        out_shape=jax.ShapeDtypeStruct((chips, 2, per, n), x.dtype),
+        input_output_aliases={3 + chips: 0} if more else {},
         compiler_params=params(),
-        name="project",
-    )(koff, x0, x1, slots, *ws)
+    )(koff, x, slots, *ws, *more)
 
 
 def unpack_rows(got, target, rows):
@@ -128,12 +118,12 @@
         grid_spec=grid_spec,
         out_shape=[jax.ShapeDtypeStruct((rows, n), got.dtype)] * 2,
         compiler_params=params(),
-        name="keys",
     )(core, got, target, cosine, sine)
 
 
 def attend_kernel(d, core, got, target, *refs):
-    *blocks, cosine, sine, qdocs, kdocs, out, q, kv = refs
+    *refs, out, q, kv = refs
+    *blocks, cosine, sine, qdocs, kdocs = refs[:7]
     rows = out.shape[0]
     heads = got.shape[-1] // HEAD
     span = rows + QT
@@ -163,9 +153,9 @@
         ok = (behind > 0) & (behind <= rows) & (
             qdocs[pl.ds(at, QT), :1] == kdocs[0, :, pl.ds(at, span)]
         )
-        s = jnp.where(ok[None], s * scale, MASKED)
+        s = jnp.where(ok[None], s, MASKED)
         top = jnp.max(s, axis=-1, keepdims=True)
-        w = jnp.exp(s - top)
+        w = jnp.exp((s - top) * scale)
         total = jnp.sum(w, axis=-1, keepdims=True)
         o = jnp.dot(
             w.astype(kv.dtype).reshape(heads * QT, span), vs, preferred_element_type=jnp.float32
@@ -175,11 +165,13 @@
             out[pl.ds(at, QT), h * HEAD : (h + 1) * HEAD] = o[h].astype(out.dtype)
         return carry
 
-    lax.fori_loop(0, rows // QT, tile, 0)
-
-
-def attend(d, core, got, target, kv3, cosine, sine, qdocs, kdocs, rows):
+    lax.fori_loop(0, rows // QT, tile, 0, unroll=2)
+
+
+def attend(d, scalars, got, target, kv3, cosine, sine, qdocs, kdocs, base=None):
     chips, _, _, cap, n = got.shape
+    rows = kv3[0].shape[0]
+    more = [] if base is None else [base]
     grid_spec = pltpu.PrefetchScalarGridSpec(
         num_scalar_prefetch=1,
         grid=(1,),
@@ -187,50 +179,52 @@
             pl.BlockSpec((chips, 2, 1, cap, n), lambda i, s: (0, 0, d, 0, 0)),
             pl.BlockSpec((1, 1, chips * 2 * cap), lambda i, s: (d, 0, 0)),
             *[pl.BlockSpec((rows, 2 * HEAD), lambda i, s: (0, 0))] * 3,
-            pl.BlockSpec((rows, HEAD), lambda i, s: (d ^ s[0], 0)),
-            pl.BlockSpec((rows, HEAD), lambda i, s: (d ^ s[0], 0)),
-            pl.BlockSpec((rows, HEAD), lambda i, s: (d ^ s[0], 0)),
+            *[pl.BlockSpec((rows, HEAD), lambda i, s: (d ^ s[0], 0))] * 3,
             pl.BlockSpec((1, 1, 2 * rows), lambda i, s: (d ^ s[0], 0, 0)),
+            *[pl.BlockSpec(memory_space=pl.ANY) for _ in more],
         ],
-        out_specs=pl.BlockSpec((rows, n), lambda i, s: (0, 0)),
+        out_specs=pl.BlockSpec((rows, n), lambda i, s: (0, s[1] if more else 0)),
         scratch_shapes=[
             pltpu.VMEM((n // HEAD, rows, HEAD), got.dtype),
             pltpu.VMEM((2 * rows, 2 * HEAD), got.dtype),
         ],
     )
+    shape = base.shape if more else (rows, n)
     return pl.pallas_call(
         functools.partial(attend_kernel, d),
         grid_spec=grid_spec,
-        out_shape=jax.ShapeDtypeStruct((rows, n), got.dtype),
+        out_shape=jax.ShapeDtypeStruct(shape, got.dtype),
+        input_output_aliases={10: 0} if more else {},
         compiler_params=params(),
-        name="attend",
-    )(core, got, target, *kv3, cosine, sine, qdocs, kdocs)
-
-
-def join_kernel(place, a, b, c, d, out):
-    i = pl.program_id(0)
-    for k, piece in enumerate((a, b, c, d)):
-
-        @pl.when(i == k)
-        def _(piece=piece):
+    )(scalars, got, target, *kv3, cosine, sine, qdocs, kdocs, *more)
+
+
+def place_kernel(count, scalars, *refs):
+    out = refs[-1]
+    for k in range(count):
+
+        @pl.when(pl.program_id(0) == k)
+        def _(piece=refs[k]):
             out[...] = piece[...]
 
 
-def join(part, pieces):
+def place(scalars, pieces, first, parts, base=None):
     rows, n = pieces[0].shape
+    more = [] if base is None else [base]
     grid_spec = pltpu.PrefetchScalarGridSpec(
         num_scalar_prefetch=1,
         grid=(len(pieces),),
-        in_specs=[pl.BlockSpec((rows, n), lambda i, s: (0, 0)) for _ in pieces],
-        out_specs=pl.BlockSpec((rows, n), lambda i, s: (0, s[0] ^ i)),
+        in_specs=[pl.BlockSpec((rows, n), lambda i, s: (0, 0)) for _ in pieces]
+        + [pl.BlockSpec(memory_space=pl.ANY) for _ in more],
+        out_specs=pl.BlockSpec((rows, n), lambda i, s: (0, s[1] ^ (i + first))),
     )
     return pl.pallas_call(
-        join_kernel,
+        functools.partial(place_kernel, len(pieces)),
         grid_spec=grid_spec,
-        out_shape=jax.ShapeDtypeStruct((rows, n * len(pieces)), pieces[0].dtype),
+        out_shape=jax.ShapeDtypeStruct((rows, n * parts), pieces[0].dtype),
+        input_output_aliases={1 + len(pieces): 0} if more else {},
         compiler_params=params(),
-        name="join",
-    )(part, *pieces)
+    )(scalars, *pieces, *more)
 
 
 def chip_cycle(chips):
@@ -251,10 +245,10 @@
     found = [shard]
     a = b = shard
     for hop in range(chips // 2):
-        a = lax.ppermute(a, "ctx", forth)
+        a = lax.ppermute(a, CTX, forth)
         found.append(a)
         if hop < (chips - 1) // 2:
-            b = lax.ppermute(b, "ctx", back)
+            b = lax.ppermute(b, CTX, back)
             found.append(b)
     return found
 
@@ -272,14 +266,14 @@
 
 def layer(hidden, dest, doc_ids, w_query, key_weight, value_weight):
     rows = hidden.shape[0]
-    dp = lax.axis_size("dp")
-    size = lax.axis_size("ctx")
+    dp = lax.axis_size(DP)
+    size = lax.axis_size(CTX)
     chips = size // 2
     cap = 2 * rows // size
-    index = lax.axis_index("ctx")
+    index = lax.axis_index(CTX)
     chip = index // 2
     core = index % 2
-    part = (lax.axis_index("dp") % 2) * 2 + core
+    part = (lax.axis_index(DP) % 2) * 2 + core
     parts = 4
     kq = w_query.shape[1] // parts
     kk = key_weight.shape[1] // parts
@@ -290,14 +284,14 @@
     same_core = [[2 * i + c for i in range(chips)] for c in range(2)]
 
     def to_core(x):
-        return lax.ppermute(x, "ctx", core_pairs)
+        return lax.ppermute(x, CTX, core_pairs)
 
     def to_side(x):
-        return lax.ppermute(x, "dp", side_pairs)
+        return lax.ppermute(x, DP, side_pairs)
 
     def exchange(x):
         return lax.all_to_all(
-            x, "ctx", split_axis=0, concat_axis=0, tiled=True, axis_index_groups=same_core
+            x, CTX, split_axis=0, concat_axis=0, tiled=True, axis_index_groups=same_core
         )
 
     ints = to_side(jnp.concatenate([dest, doc_ids]))
@@ -313,7 +307,9 @@
             axis=1,
         )
 
-    shard = jnp.concatenate([columns(part), to_core(columns(part ^ 1))], axis=0)
+    theirs = columns(part ^ 1)
+    theirs = to_core(theirs)
+    shard = jnp.concatenate([columns(part), theirs], axis=0)
     ws_kv = ring_gather(shard[:, : 2 * kk], chips)
     ws_q = ring_gather(shard[:, 2 * kk :], chips)
     sources = ring_sources(chip, chips)
@@ -328,11 +324,12 @@
     both = jnp.stack([dest, ints[:rows]])
     tables = lax.all_to_all(
         jnp.broadcast_to(both[None], (size, 2, rows)),
-        "ctx",
+        CTX,
         split_axis=0,
         concat_axis=0,
         tiled=True,
     )
+    tables, _ = lax.optimization_barrier((tables, ws_kv[4]))
     tables = jnp.moveaxis(tables, 1, 0).reshape(2, chips, 2, rows)
     tables = jnp.where(core == 0, tables, tables[:, :, ::-1])
     block = tables // rows
@@ -369,7 +366,7 @@
     cos_half, sin_half = jnp.cos(angles), jnp.sin(angles)
     cosine = jnp.concatenate([cos_half, cos_half], axis=1)
     sine = jnp.concatenate([-sin_half, sin_half], axis=1)
-    core_ref = core.reshape(1).astype(jnp.int32)
+    scalars = jnp.stack([core, part]).astype(jnp.int32)
 
     def doc_tables(docs):
         padded = jnp.concatenate([jnp.full((rows,), -1, jnp.int32), docs])
@@ -382,38 +379,44 @@
     ahead = [(i, i + 2) for i in range(size - 2)]
 
     def send(t, ws):
-        out = project(*xs[t], slots[t], ws, koff, 2 * cap)
+        out = None
+        for i, x in enumerate(xs[t]):
+            out = project(x, slots[t], ws, koff, 2 * cap, i, out)
         got = exchange(out.reshape(chips, 4 * cap, out.shape[-1]))
         return got.reshape(chips, 2, 2, cap, out.shape[-1])
 
     def keys_of(t, got):
-        first, second = unpack_keys(core_ref, got, targets[t], cosine, sine, rows)
-        return lax.ppermute(second, "ctx", ahead), first, second
-
-    def result(t, d, got, kv3):
-        return attend(d, core_ref, got, targets[t], kv3, cosine, sine, *docs[t], rows)
+        first, second = unpack_keys(scalars, got, targets[t], cosine, sine, rows)
+        return lax.ppermute(second, CTX, ahead), first, second
+
+    def result(t, d, got, kv3, base=None):
+        return attend(d, scalars, got, targets[t], kv3, cosine, sine, *docs[t], base)
 
     kv_own = keys_of(0, send(0, ws_kv))
     kv_side = keys_of(1, send(1, ws_kv))
     got_side = send(1, ws_q)
     got_own = send(0, ws_q)
-    far = to_side(result(1, 1, got_side, kv_side))
+    far = result(1, 1, got_side, kv_side)
+    far = to_side(far)
     far = to_core(far)
-    near = to_side(result(1, 0, got_side, kv_side))
-    other = to_core(result(0, 1, got_own, kv_own))
-    own = result(0, 0, got_own, kv_own)
-    return join(part.reshape(1).astype(jnp.int32), (own, other, near, far))
+    near = result(1, 0, got_side, kv_side)
+    near = to_side(near)
+    base = place(scalars, (near, far), 2, parts)
+    other = result(0, 1, got_own, kv_own)
+    other = to_core(other)
+    base = result(0, 0, got_own, kv_own, base)
+    return place(scalars, (other,), 1, parts, base)
 
 
 def solution(mesh):
     placed = (
-        P(("dp", "ctx"), None),
-        P(("dp", "ctx")),
-        P("dp"),
-        P("ctx", None),
-        P("ctx", None),
-        P("ctx", None),
+        P((DP, CTX), None),
+        P((DP, CTX)),
+        P(DP),
+        P(CTX, None),
+        P(CTX, None),
+        P(CTX, None),
     )
     return jax.shard_map(
-        layer, mesh=mesh, in_specs=placed, out_specs=P(("dp", "ctx"), None), check_vma=False
-    )
+        layer, mesh=mesh, in_specs=placed, out_specs=P((DP, CTX), None), check_vma=False
+    )

time: 424 us -> 424 us (level)
  the two profiles are of different devices: /device:TPU:16 before, /device:TPU:12 now
where the time goes in v1:
time: 424 us; the launch traced here: 423 us
  waiting for transfers between devices  243 us (57%)
  Pallas kernels  96.1 us (23%)
  starting transfers between devices  58.9 us (14%)
  local copies, waits for them, and re-layouts  15.4 us (4%)
  other arithmetic  8.08 us (2%)
    ppermute x4, waiting for transfers between devices, to_side(): return lax.ppermute(x, DP, side_pairs)  93.4 us
    pallas_call x8, Pallas kernels, project(): pl.pallas_call(project_kernel, grid_spec=grid_spec, out_shape=jax.ShapeDt...  53.1 us
    ppermute x6, waiting for transfers between devices, ring_gather(): b = lax.ppermute(b, CTX, back)  37.8 us
    all_to_all x4, waiting for transfers between devices, exchange(): lax.all_to_all(x, CTX, split_axis=0, concat_axis=0, tiled=True, axis_inde...  37.5 us
    ppermute x2, waiting for transfers between devices, keys_of(): return (lax.ppermute(second, CTX, ahead), first, second)  35.7 us
    ppermute x8, waiting for transfers between devices, ring_gather(): a = lax.ppermute(a, CTX, forth)  33.2 us
    pallas_call x4, Pallas kernels, attend(): pl.pallas_call(functools.partial(attend_kernel, d), grid_spec=grid_spec,...  30 us
    all_to_all x4, starting transfers between devices, exchange(): lax.all_to_all(x, CTX, split_axis=0, concat_axis=0, tiled=True, axis_inde...  23.5 us
  transfers between devices with their start and end apart: 30, of which 18 were waited for; matrix products, arithmetic and copies ran while one was open for 4% of the time, Pallas kernels for 22%

profile of v1, /device:TPU:12, one launch (start us, length us, event | category | flops | bytes accessed | tf_op | source)
XLA Modules:
  0.0 422.8 jit_solution(3623211786680717844)
XLA Ops:
  0.0 1.6 collective-permute-start.19
  2.6 90.1 %collective-permute-done.19.x = bf16[512,4096]{1,0:T(8,128)(2,1)} collective-permute-done((bf16[512,4096]{1,0:T(8,128)(2,1)}, bf16[512,4096]{1,0:T(8,128)(2,1)}, u32[]{:S(2)}, u32[]{:S(2)}) %collective-permute-start.19) | collective-permute-done | bytes 4194336 | tf_op jit(solution)/shard_map/ppermute | solution.py:290
  94.3 1.6 collective-permute-start.1
  96.5 4.1 collective-permute-done.2
  100.7 1.6 collective-permute-start.3
  104.8 6.2 %all-to-all-start = ((s32[16,2,512]{2,1,0:T(2,128)}), s32[16,2,512]{2,1,0:T(2,128)S(1)}, u32[]{:S(2)}, u32[]{:S(2)}) async-start(s32[16,2,512]{2,1,0:T(2,128)} %broadcast_in_dim.34), calls=%async_computation | async-start | bytes 131072 | tf_op jit(solution)/shard_map/all_to_all | solution.py:325
  113.8 1.7 all-to-all-done
  115.5 4.0 collective-permute-done.4.refs_4_
  124.0 4.5 %collective-permute-done.14.refs_5_ = bf16[512,256]{1,0:T(8,128)(2,1)S(1)} collective-permute-done((bf16[512,256]{1,0:T(8,128)(2,1)S(1)}, bf16[512,256]{1,0:T(8,128)(2,1)S(1)}, u32[]{:S(2)}, u32[]{:S(2)}) %collective-permute-start.14) | collective-permute-done | bytes 262176 | tf_op jit(solution)/shard_map/ppermute | solution.py:248
  129.9 5.4 %collective-permute-done.16.refs_7_ = bf16[512,256]{1,0:T(8,128)(2,1)S(1)} collective-permute-done((bf16[512,256]{1,0:T(8,128)(2,1)S(1)}, bf16[512,256]{1,0:T(8,128)(2,1)S(1)}, u32[]{:S(2)}, u32[]{:S(2)}) %collective-permute-start.16) | collective-permute-done | bytes 262176 | tf_op jit(solution)/shard_map/ppermute | solution.py:248
  136.0 5.6 %shard_map.84.refs_8_ = bf16[8,2,128,256]{3,2,1,0:T(8,128)(2,1)} custom-call(s32[16]{0:T(128)} %mul.90.koff, bf16[512,4096]{1,0:T(8,128)(2,1)} %x.7, s32[2,1,512]{2,1,0:T(1,128)} %get-tuple-element.30.slots, bf16[512,256]{1,0:T(8,128)(2,1)} %copy-done.11, bf16[512,256]{1,0:T(8,128)(2,1)} %copy-done.13, bf16[512,256]{1,0:T(8,128)(2,1)} %copy-done.12, ...), custom_call_target="tpu_custom_call" | custom-call | tf_op jit(solution)/shard_map/pallas_call | solution.py:72
  141.6 5.6 %shard_map.85 = bf16[8,2,128,256]{3,2,1,0:T(8,128)(2,1)} custom-call(s32[16]{0:T(128)} %mul.90.koff, bf16[512,4096]{1,0:T(8,128)(2,1)} %collective-permute-done.x, s32[2,1,512]{2,1,0:T(1,128)} %get-tuple-element.30.slots, bf16[512,256]{1,0:T(8,128)(2,1)} %copy-done.11, bf16[512,256]{1,0:T(8,128)(2,1)} %copy-done.13, ...), custom_call_target="tpu_custom_call", output_to_operand_aliasing={{}: (11, {})} | custom-call | tf_op jit(solution)/shard_map/pallas_call | solution.py:72
  147.2 4.9 %all-to-all-start.2 = ((bf16[8,256,256]{2,1,0:T(8,128)(2,1)}), bf16[8,256,256]{2,1,0:T(8,128)(2,1)S(1)}, u32[]{:S(2)}, u32[]{:S(2)}) async-start(bf16[8,256,256]{2,1,0:T(8,128)(2,1)} %bitcast.62), calls=%async_computation.2 | async-start | bytes 2097152 | tf_op jit(solution)/shard_map/all_to_all | solution.py:293
  152.8 5.6 %shard_map.90.refs_8_ = bf16[8,2,128,256]{3,2,1,0:T(8,128)(2,1)} custom-call(s32[16]{0:T(128)} %mul.90.koff, bf16[512,4096]{1,0:T(8,128)(2,1)} %collective-permute-done.19.x, s32[2,1,512]{2,1,0:T(1,128)} %get-tuple-element.29.slots, bf16[512,256]{1,0:T(8,128)(2,1)} %copy-done.11, bf16[512,256]{1,0:T(8,128)(2,1)} %copy-done.13, bf16[512,256]{1,0:T(8,128)(2,1)} %copy-done.12, ...), custom_call_target="tpu_custom_call" | custom-call | tf_op jit(solution)/shard_map/pallas_call | solution.py:72
  158.3 5.6 %shard_map.91 = bf16[8,2,128,256]{3,2,1,0:T(8,128)(2,1)} custom-call(s32[16]{0:T(128)} %mul.90.koff, bf16[512,4096]{1,0:T(8,128)(2,1)} %collective-permute-done.20.x, s32[2,1,512]{2,1,0:T(1,128)} %get-tuple-element.29.slots, bf16[512,256]{1,0:T(8,128)(2,1)} %copy-done.11, bf16[512,256]{1,0:T(8,128)(2,1)} %copy-done.13, ...), custom_call_target="tpu_custom_call", output_to_operand_aliasing={{}: (11, {})} | custom-call | tf_op jit(solution)/shard_map/pallas_call | solution.py:72
  163.9 9.2 %all-to-all-done.2 = bf16[8,256,256]{2,1,0:T(8,128)(2,1)S(1)} async-done(((bf16[8,256,256]{2,1,0:T(8,128)(2,1)}), bf16[8,256,256]{2,1,0:T(8,128)(2,1)S(1)}, u32[]{:S(2)}, u32[]{:S(2)}) %all-to-all-start.2) | async-done | bytes 1048608 | tf_op jit(solution)/shard_map/all_to_all | solution.py:293
  173.1 7.4 %all-to-all-start.4 = ((bf16[8,256,256]{2,1,0:T(8,128)(2,1)}), bf16[8,256,256]{2,1,0:T(8,128)(2,1)}, u32[]{:S(2)}, u32[]{:S(2)}) async-start(bf16[8,256,256]{2,1,0:T(8,128)(2,1)} %bitcast.61), calls=%async_computation.4 | async-start | bytes 2097152 | tf_op jit(solution)/shard_map/all_to_all | solution.py:293
  182.0 13.2 %collective-permute-done.5.refs_1_ = bf16[512,512]{1,0:T(8,128)(2,1)S(1)} collective-permute-done((bf16[512,512]{1,0:T(8,128)(2,1)S(1)}, bf16[512,512]{1,0:T(8,128)(2,1)S(1)}, u32[]{:S(2)}, u32[]{:S(2)}) %collective-permute-start.5) | collective-permute-done | bytes 524320 | tf_op jit(solution)/shard_map/ppermute | solution.py:248
  195.2 18.0 %collective-permute-done.6.refs_2_ = bf16[512,512]{1,0:T(8,128)(2,1)S(1)} collective-permute-done((bf16[512,512]{1,0:T(8,128)(2,1)S(1)}, bf16[512,512]{1,0:T(8,128)(2,1)S(1)}, u32[]{:S(2)}, u32[]{:S(2)}) %collective-permute-start.6) | collective-permute-done | bytes 524320 | tf_op jit(solution)/shard_map/ppermute | solution.py:251
  213.2 2.5 collective-permute-start.8
  215.7 3.8 collective-permute-done.7.refs_3_
  219.5 7.6 %collective-permute-done.8.refs_4_ = bf16[512,512]{1,0:T(8,128)(2,1)S(1)} collective-permute-done((bf16[512,512]{1,0:T(8,128)(2,1)S(1)}, bf16[512,512]{1,0:T(8,128)(2,1)S(1)}, u32[]{:S(2)}, u32[]{:S(2)}) %collective-permute-start.8) | collective-permute-done | bytes 524320 | tf_op jit(solution)/shard_map/ppermute | solution.py:251
  227.1 2.5 collective-permute-start.10
  229.5 2.0 collective-permute-done.9.refs_5_
  231.8 8.2 %collective-permute-done.10.refs_6_ = bf16[512,512]{1,0:T(8,128)(2,1)S(1)} collective-permute-done((bf16[512,512]{1,0:T(8,128)(2,1)S(1)}, bf16[512,512]{1,0:T(8,128)(2,1)S(1)}, u32[]{:S(2)}, u32[]{:S(2)}) %collective-permute-start.10) | collective-permute-done | bytes 524320 | tf_op jit(solution)/shard_map/ppermute | solution.py:251
  240.0 2.7 collective-permute-done.11.refs_7_
  243.6 7.7 %shard_map.88.refs_8_ = bf16[8,2,128,512]{3,2,1,0:T(8,128)(2,1)} custom-call(s32[16]{0:T(128)} %mul.90.koff, bf16[512,4096]{1,0:T(8,128)(2,1)} %collective-permute-done.19.x, s32[2,1,512]{2,1,0:T(1,128)} %get-tuple-element.29.slots, bf16[512,512]{1,0:T(8,128)(2,1)} %copy-done.3, bf16[512,512]{1,0:T(8,128)(2,1)} %copy-done.4, bf16[512,512]{1,0:T(8,128)(2,1)} %copy-done.5, ...), custom_call_target="tpu_custom_call" | custom-call | tf_op jit(solution)/shard_map/pallas_call | solution.py:72
  251.3 7.7 %shard_map.89 = bf16[8,2,128,512]{3,2,1,0:T(8,128)(2,1)} custom-call(s32[16]{0:T(128)} %mul.90.koff, bf16[512,4096]{1,0:T(8,128)(2,1)} %collective-permute-done.20.x, s32[2,1,512]{2,1,0:T(1,128)} %get-tuple-element.29.slots, bf16[512,512]{1,0:T(8,128)(2,1)} %copy-done.3, bf16[512,512]{1,0:T(8,128)(2,1)} %copy-done.4, ...), custom_call_target="tpu_custom_call", output_to_operand_aliasing={{}: (11, {})} | custom-call | tf_op jit(solution)/shard_map/pallas_call | solution.py:72
  259.0 4.2 all-to-all-start.3
  263.2 7.7 %shard_map.82.refs_8_ = bf16[8,2,128,512]{3,2,1,0:T(8,128)(2,1)} custom-call(s32[16]{0:T(128)} %mul.90.koff, bf16[512,4096]{1,0:T(8,128)(2,1)} %x.7, s32[2,1,512]{2,1,0:T(1,128)} %get-tuple-element.30.slots, bf16[512,512]{1,0:T(8,128)(2,1)} %copy-done.3, bf16[512,512]{1,0:T(8,128)(2,1)} %copy-done.4, bf16[512,512]{1,0:T(8,128)(2,1)} %copy-done.5, ...), custom_call_target="tpu_custom_call" | custom-call | tf_op jit(solution)/shard_map/pallas_call | solution.py:72
  270.9 7.7 %shard_map.83 = bf16[8,2,128,512]{3,2,1,0:T(8,128)(2,1)} custom-call(s32[16]{0:T(128)} %mul.90.koff, bf16[512,4096]{1,0:T(8,128)(2,1)} %collective-permute-done.x, s32[2,1,512]{2,1,0:T(1,128)} %get-tuple-element.30.slots, bf16[512,512]{1,0:T(8,128)(2,1)} %copy-done.3, bf16[512,512]{1,0:T(8,128)(2,1)} %copy-done.4, ...), custom_call_target="tpu_custom_call", output_to_operand_aliasing={{}: (11, {})} | custom-call | tf_op jit(solution)/shard_map/pallas_call | solution.py:72
  278.6 28.3 %all-to-all-done.3 = bf16[8,256,512]{2,1,0:T(8,128)(2,1)S(1)} async-done(((bf16[8,256,512]{2,1,0:T(8,128)(2,1)}), bf16[8,256,512]{2,1,0:T(8,128)(2,1)S(1)}, u32[]{:S(2)}, u32[]{:S(2)}) %all-to-all-start.3) | async-done | bytes 2097184 | tf_op jit(solution)/shard_map/all_to_all | solution.py:293
  308.2 6.9 %all-to-all-start.1 = ((bf16[8,256,512]{2,1,0:T(8,128)(2,1)}), bf16[8,256,512]{2,1,0:T(8,128)(2,1)S(1)}, u32[]{:S(2)}, u32[]{:S(2)}) async-start(bf16[8,256,512]{2,1,0:T(8,128)(2,1)} %bitcast.59), calls=%async_computation.1 | async-start | bytes 4194304 | tf_op jit(solution)/shard_map/all_to_all | solution.py:293
  315.8 1.9 fusion.7
  319.6 1.9 select_reduce_fusion
  322.2 3.8 shard_map.92
  326.0 3.4 collective-permute-start.21
  330.2 35.7 %collective-permute-done.21.refs_0_ = bf16[512,256]{1,0:T(8,128)(2,1)S(1)} collective-permute-done((bf16[512,256]{1,0:T(8,128)(2,1)}, bf16[512,256]{1,0:T(8,128)(2,1)S(1)}, u32[]{:S(2)}, u32[]{:S(2)}) %collective-permute-start.21) | collective-permute-done | bytes 262176 | tf_op jit(solution)/shard_map/ppermute | solution.py:390
  366.9 7.5 %shard_map.94 = bf16[512,512]{1,0:T(8,128)(2,1)} custom-call(s32[2]{0:T(128)} %pad_add_fusion.4.core.scalars, bf16[8,2,2,64,512]{4,3,2,1,0:T(8,128)(2,1)} %bitcast.57, s32[2,1,1024]{2,1,0:T(1,128)} %squeeze.30.target, bf16[512,256]{1,0:T(8,128)(2,1)} %copy-done.21, bf16[512,256]{1,0:T(8,128)(2,1)} %get-tuple-element.14.refs_1_, ...), custom_call_target="tpu_custom_call" | custom-call | tf_op jit(solution)/shard_map/pallas_call | solution.py:193
  374.4 1.5 collective-permute-start.23
  376.6 3.8 shard_map.86
  380.4 5.4 %collective-permute-start.17 = (bf16[512,256]{1,0:T(8,128)(2,1)}, bf16[512,256]{1,0:T(8,128)(2,1)S(1)}, u32[]{:S(2)}, u32[]{:S(2)}) collective-permute-start(bf16[512,256]{1,0:T(8,128)(2,1)} %get-tuple-element.11.refs_2_), channel_id=1, source_target_pairs={{0,2},{1,3},{2,4},{3,5},{4,6},{5,7},{6,8},{7,9},{8,10},{9,11},{10,... | collective-permute-start | bytes 786440 | tf_op jit(solution)/shard_map/ppermute | solution.py:390
  386.5 7.5 %shard_map.93 = bf16[512,512]{1,0:T(8,128)(2,1)} custom-call(s32[2]{0:T(128)} %pad_add_fusion.4.core.scalars, bf16[8,2,2,64,512]{4,3,2,1,0:T(8,128)(2,1)} %bitcast.58, s32[2,1,1024]{2,1,0:T(1,128)} %squeeze.30.target, bf16[512,256]{1,0:T(8,128)(2,1)} %copy-done.21, bf16[512,256]{1,0:T(8,128)(2,1)} %get-tuple-element.14.refs_1_, ...), custom_call_target="tpu_custom_call" | custom-call | tf_op jit(solution)/shard_map/pallas_call | solution.py:193
  396.1 7.5 %shard_map.87 = bf16[512,512]{1,0:T(8,128)(2,1)} custom-call(s32[2]{0:T(128)} %pad_add_fusion.4.core.scalars, bf16[8,2,2,64,512]{4,3,2,1,0:T(8,128)(2,1)} %bitcast.55, s32[2,1,1024]{2,1,0:T(1,128)} %squeeze.14.target, bf16[512,256]{1,0:T(8,128)(2,1)} %copy-done.20, bf16[512,256]{1,0:T(8,128)(2,1)} %get-tuple-element.12.refs_1_, ...), custom_call_target="tpu_custom_call" | custom-call | tf_op jit(solution)/shard_map/pallas_call | solution.py:193
  404.1 3.4 collective-permute-done.22.refs_0_
  409.1 2.9 shard_map.95.refs_7_
  412.0 7.5 %shard_map.96.refs_1_ = bf16[512,2048]{1,0:T(8,128)(2,1)} custom-call(s32[2]{0:T(128)} %pad_add_fusion.4.core.scalars, bf16[8,2,2,64,512]{4,3,2,1,0:T(8,128)(2,1)} %bitcast.56, s32[2,1,1024]{2,1,0:T(1,128)} %squeeze.14.target, bf16[512,256]{1,0:T(8,128)(2,1)} %copy-done.20, ...), custom_call_target="tpu_custom_call", output_to_operand_aliasing={{}: (10, {})} | custom-call | tf_op jit(solution)/shard_map/pallas_call | solution.py:193
  420.3 2.5 shard_map.97
  (145 shorter events, 30.9 us)
Async XLA Ops:
  0.0 95.9 %copy-start = (s32[8]{0:T(128)S(1)}, s32[8]{0:T(128)}, u32[]{:S(2)}) copy-start(s32[8]{0:T(128)} %constant.131.clone) | copy-start | bytes 100
  0.0 102.8 %copy-start.33 = (s32[8]{0:T(128)S(1)}, s32[8]{0:T(128)}, u32[]{:S(2)}) copy-start(s32[8]{0:T(128)} %constant.132.clone) | copy-start | bytes 100
  0.0 94.3 %copy-start.28 = (s32[8192]{0:T(1024)S(1)}, s32[8192]{0:T(1024)}, u32[]{:S(2)}) copy-start(s32[8192]{0:T(1024)} %param.10) | copy-start | bytes 98308
  0.0 94.3 %copy-start.32 = (s32[512]{0:T(512)S(1)}, s32[512]{0:T(512)}, u32[]{:S(2)}) copy-start(s32[512]{0:T(512)} %param.9) | copy-start | bytes 6148
  0.0 92.7 %collective-permute-start.19 = (bf16[512,4096]{1,0:T(8,128)(2,1)}, bf16[512,4096]{1,0:T(8,128)(2,1)}, u32[]{:S(2)}, u32[]{:S(2)}) collective-permute-start(bf16[512,4096]{1,0:T(8,128)(2,1)} %x.7), channel_id=1, source_target_pairs={{0,16},{16,0},{1,17},{17,1},{2,18},{18,2},{3,19},{19,3},{4,20},{20... | collective-permute-start | bytes 12582920 | tf_op jit(solution)/shard_map/ppermute | solution.py:290
  1.6 140.0 %collective-permute-start = (bf16[512,4096]{1,0:T(8,128)(2,1)}, bf16[512,4096]{1,0:T(8,128)(2,1)}, u32[]{:S(2)}, u32[]{:S(2)}) collective-permute-start(bf16[512,4096]{1,0:T(8,128)(2,1)} %x.7), channel_id=1, source_target_pairs={{0,1},{1,0},{2,3},{3,2},{4,5},{5,4},{6,7},{7,6},{8,9},{9,8},{10,11... | collective-permute-start | bytes 12582920 | tf_op jit(solution)/shard_map/ppermute | solution.py:287
  92.7 65.6 %collective-permute-start.20 = (bf16[512,4096]{1,0:T(8,128)(2,1)}, bf16[512,4096]{1,0:T(8,128)(2,1)}, u32[]{:S(2)}, u32[]{:S(2)}) collective-permute-start(bf16[512,4096]{1,0:T(8,128)(2,1)} %collective-permute-done.19.x), channel_id=1, source_target_pairs={{0,1},{1,0},{2,3},{3,2},{4,5},{5,4},{6,7},{7,6},{8,9},{9,8},{10,11... | collective-permute-start | bytes 12582920 | tf_op jit(solution)/shard_map/ppermute | solution.py:287
  93.7 6.9 %collective-permute-start.2 = (bf16[256,768]{1,0:T(8,128)(2,1)S(1)}, bf16[256,768]{1,0:T(8,128)(2,1)S(1)}, u32[]{:S(2)}, u32[]{:S(2)}) collective-permute-start(bf16[256,768]{1,0:T(8,128)(2,1)S(1)} %pad_maximum_fusion.5), channel_id=1, source_target_pairs={{0,1},{1,0},{2,3},{3,2},{4,5},{5,4},{6,7},{7,6},{8,9},{9,8},{10,11... | collective-permute-start | bytes 1179656 | tf_op jit(solution)/shard_map/ppermute | solution.py:287
  94.3 9.8 %collective-permute-start.1 = (s32[8704]{0:T(1024)S(1)}, s32[8704]{0:T(1024)S(1)}, u32[]{:S(2)}, u32[]{:S(2)}) collective-permute-start(s32[8704]{0:T(1024)S(1)} %pad_add_fusion), channel_id=1, source_target_pairs={{0,16},{16,0},{1,17},{17,1},{2,18},{18,2},{3,19},{19,3},{4,20},{20... | collective-permute-start | bytes 104456 | tf_op jit(solution)/shard_map/ppermute | solution.py:290
  100.7 34.6 %copy-start.11 = (bf16[512,256]{1,0:T(8,128)(2,1)}, bf16[512,256]{1,0:T(8,128)(2,1)S(1)}, u32[]{:S(2)}) copy-start(bf16[512,256]{1,0:T(8,128)(2,1)S(1)} %pad_maximum_fusion.6.refs_0_) | copy-start | bytes 786436
  100.7 10.3 %collective-permute-start.3 = (bf16[512,256]{1,0:T(8,128)(2,1)S(1)}, bf16[512,256]{1,0:T(8,128)(2,1)S(1)}, u32[]{:S(2)}, u32[]{:S(2)}) collective-permute-start(bf16[512,256]{1,0:T(8,128)(2,1)S(1)} %pad_maximum_fusion.6.refs_0_), channel_id=1, source_target_pairs={{0,2},{1,3},{4,0},{5,1},{8,4},{9,5},{12,8},{13,9},{14,12},{15,13},... | collective-permute-start | bytes 786440 | tf_op jit(solution)/shard_map/ppermute | solution.py:251
  102.3 10.2 %collective-permute-start.12 = (bf16[512,256]{1,0:T(8,128)(2,1)S(1)}, bf16[512,256]{1,0:T(8,128)(2,1)S(1)}, u32[]{:S(2)}, u32[]{:S(2)}) collective-permute-start(bf16[512,256]{1,0:T(8,128)(2,1)S(1)} %pad_maximum_fusion.6.refs_0_), channel_id=1, source_target_pairs={{0,4},{1,5},{4,8},{5,9},{8,12},{9,13},{12,14},{13,15},{14,10},{15,... | collective-permute-start | bytes 786440 | tf_op jit(solution)/shard_map/ppermute | solution.py:248
  104.1 19.9 %copy-start.30 = (s32[8704]{0:T(1024)}, s32[8704]{0:T(1024)S(1)}, u32[]{:S(2)}) copy-start(s32[8704]{0:T(1024)S(1)} %collective-permute-done.1) | copy-start | bytes 104452
  104.8 10.7 %all-to-all-start = ((s32[16,2,512]{2,1,0:T(2,128)}), s32[16,2,512]{2,1,0:T(2,128)S(1)}, u32[]{:S(2)}, u32[]{:S(2)}) async-start(s32[16,2,512]{2,1,0:T(2,128)} %broadcast_in_dim.34), calls=%async_computation | async-start | bytes 131072 | tf_op jit(solution)/shard_map/all_to_all | solution.py:325
  111.0 24.3 %copy-start.12 = (bf16[512,256]{1,0:T(8,128)(2,1)}, bf16[512,256]{1,0:T(8,128)(2,1)S(1)}, u32[]{:S(2)}) copy-start(bf16[512,256]{1,0:T(8,128)(2,1)S(1)} %collective-permute-done.3.refs_2_) | copy-start | bytes 786436
  111.0 8.4 %collective-permute-start.4 = (bf16[512,256]{1,0:T(8,128)(2,1)S(1)}, bf16[512,256]{1,0:T(8,128)(2,1)S(1)}, u32[]{:S(2)}, u32[]{:S(2)}) collective-permute-start(bf16[512,256]{1,0:T(8,128)(2,1)S(1)} %collective-permute-done.3.refs_2_), channel_id=1, source_target_pairs={{0,2},{1,3},{4,0},{5,1},{8,4},{9,5},{12,8},{13,9},{14,12},{15,13},... | collective-permute-start | bytes 786440 | tf_op jit(solution)/shard_map/ppermute | solution.py:251
  112.5 22.8 %copy-start.13 = (bf16[512,256]{1,0:T(8,128)(2,1)}, bf16[512,256]{1,0:T(8,128)(2,1)S(1)}, u32[]{:S(2)}) copy-start(bf16[512,256]{1,0:T(8,128)(2,1)S(1)} %collective-permute-done.12.refs_1_) | copy-start | bytes 786436
  112.6 8.4 %collective-permute-start.13 = (bf16[512,256]{1,0:T(8,128)(2,1)S(1)}, bf16[512,256]{1,0:T(8,128)(2,1)S(1)}, u32[]{:S(2)}, u32[]{:S(2)}) collective-permute-start(bf16[512,256]{1,0:T(8,128)(2,1)S(1)} %collective-permute-done.12.refs_1_), channel_id=1, source_target_pairs={{0,4},{1,5},{4,8},{5,9},{8,12},{9,13},{12,14},{13,15},{14,10},{15,... | collective-permute-start | bytes 786440 | tf_op jit(solution)/shard_map/ppermute | solution.py:248
  119.5 15.9 %copy-start.14 = (bf16[512,256]{1,0:T(8,128)(2,1)}, bf16[512,256]{1,0:T(8,128)(2,1)S(1)}, u32[]{:S(2)}) copy-start(bf16[512,256]{1,0:T(8,128)(2,1)S(1)} %collective-permute-done.4.refs_4_) | copy-start | bytes 786436
  121.0 14.3 %copy-start.15 = (bf16[512,256]{1,0:T(8,128)(2,1)}, bf16[512,256]{1,0:T(8,128)(2,1)S(1)}, u32[]{:S(2)}) copy-start(bf16[512,256]{1,0:T(8,128)(2,1)S(1)} %collective-permute-done.13.refs_3_) | copy-start | bytes 786436
  121.0 7.6 %collective-permute-start.14 = (bf16[512,256]{1,0:T(8,128)(2,1)S(1)}, bf16[512,256]{1,0:T(8,128)(2,1)S(1)}, u32[]{:S(2)}, u32[]{:S(2)}) collective-permute-start(bf16[512,256]{1,0:T(8,128)(2,1)S(1)} %collective-permute-done.13.refs_3_), channel_id=1, source_target_pairs={{0,4},{1,5},{4,8},{5,9},{8,12},{9,13},{12,14},{13,15},{14,10},{15,... | collective-permute-start | bytes 786440 | tf_op jit(solution)/shard_map/ppermute | solution.py:248
  122.4 19.2 %copy-start.25 = (s32[2,8,2,512]{3,1,2,0:T(8,128)}, s32[2,8,2,512]{3,1,2,0:T(8,128)S(1)}, u32[]{:S(2)}) copy-start(s32[2,8,2,512]{3,1,2,0:T(8,128)S(1)} %get-tuple-element.22) | copy-start | bytes 196612
  122.4 7.5 %collective-permute-start.15 = (bf16[512,256]{1,0:T(8,128)(2,1)S(1)}, bf16[512,256]{1,0:T(8,128)(2,1)S(1)}, u32[]{:S(2)}, u32[]{:S(2)}) collective-permute-start(bf16[512,256]{1,0:T(8,128)(2,1)S(1)} %collective-permute-done.4.refs_4_), channel_id=1, source_target_pairs={{0,2},{1,3},{4,0},{5,1},{8,4},{9,5},{12,8},{13,9},{14,12},{15,13},... | collective-permute-start | bytes 786440 | tf_op jit(solution)/shard_map/ppermute | solution.py:251
  128.6 6.7 %collective-permute-start.16 = (bf16[512,256]{1,0:T(8,128)(2,1)S(1)}, bf16[512,256]{1,0:T(8,128)(2,1)S(1)}, u32[]{:S(2)}, u32[]{:S(2)}) collective-permute-start(bf16[512,256]{1,0:T(8,128)(2,1)S(1)} %collective-permute-done.14.refs_5_), channel_id=1, source_target_pairs={{0,4},{1,5},{4,8},{5,9},{8,12},{9,13},{12,14},{13,15},{14,10},{15,... | collective-permute-start | bytes 786440 | tf_op jit(solution)/shard_map/ppermute | solution.py:248
  147.2 26.0 %all-to-all-start.2 = ((bf16[8,256,256]{2,1,0:T(8,128)(2,1)}), bf16[8,256,256]{2,1,0:T(8,128)(2,1)S(1)}, u32[]{:S(2)}, u32[]{:S(2)}) async-start(bf16[8,256,256]{2,1,0:T(8,128)(2,1)} %bitcast.62), calls=%async_computation.2 | async-start | bytes 2097152 | tf_op jit(solution)/shard_map/all_to_all | solution.py:293
  152.1 28.4 %copy-start.3 = (bf16[512,512]{1,0:T(8,128)(2,1)}, bf16[512,512]{1,0:T(8,128)(2,1)S(1)}, u32[]{:S(2)}) copy-start(bf16[512,512]{1,0:T(8,128)(2,1)S(1)} %pad_maximum_fusion.refs_0_) | copy-start | bytes 1572868
  152.1 43.1 %collective-permute-start.5 = (bf16[512,512]{1,0:T(8,128)(2,1)S(1)}, bf16[512,512]{1,0:T(8,128)(2,1)S(1)}, u32[]{:S(2)}, u32[]{:S(2)}) collective-permute-start(bf16[512,512]{1,0:T(8,128)(2,1)S(1)} %pad_maximum_fusion.refs_0_), channel_id=1, source_target_pairs={{0,4},{1,5},{4,8},{5,9},{8,12},{9,13},{12,14},{13,15},{14,10},{15,... | collective-permute-start | bytes 1572872 | tf_op jit(solution)/shard_map/ppermute | solution.py:248
  173.1 85.9 %all-to-all-start.4 = ((bf16[8,256,256]{2,1,0:T(8,128)(2,1)}), bf16[8,256,256]{2,1,0:T(8,128)(2,1)}, u32[]{:S(2)}, u32[]{:S(2)}) async-start(bf16[8,256,256]{2,1,0:T(8,128)(2,1)} %bitcast.61), calls=%async_computation.4 | async-start | bytes 2097152 | tf_op jit(solution)/shard_map/all_to_all | solution.py:293
  180.6 32.6 %collective-permute-start.6 = (bf16[512,512]{1,0:T(8,128)(2,1)S(1)}, bf16[512,512]{1,0:T(8,128)(2,1)S(1)}, u32[]{:S(2)}, u32[]{:S(2)}) collective-permute-start(bf16[512,512]{1,0:T(8,128)(2,1)S(1)} %pad_maximum_fusion.refs_0_), channel_id=1, source_target_pairs={{0,2},{1,3},{4,0},{5,1},{8,4},{9,5},{12,8},{13,9},{14,12},{15,13},... | collective-permute-start | bytes 1572872 | tf_op jit(solution)/shard_map/ppermute | solution.py:251
  195.2 47.6 %copy-start.4 = (bf16[512,512]{1,0:T(8,128)(2,1)}, bf16[512,512]{1,0:T(8,128)(2,1)S(1)}, u32[]{:S(2)}) copy-start(bf16[512,512]{1,0:T(8,128)(2,1)S(1)} %collective-permute-done.5.refs_1_) | copy-start | bytes 1572868
  195.2 24.2 %collective-permute-start.7 = (bf16[512,512]{1,0:T(8,128)(2,1)S(1)}, bf16[512,512]{1,0:T(8,128)(2,1)S(1)}, u32[]{:S(2)}, u32[]{:S(2)}) collective-permute-start(bf16[512,512]{1,0:T(8,128)(2,1)S(1)} %collective-permute-done.5.refs_1_), channel_id=1, source_target_pairs={{0,4},{1,5},{4,8},{5,9},{8,12},{9,13},{12,14},{13,15},{14,10},{15,... | collective-permute-start | bytes 1572872 | tf_op jit(solution)/shard_map/ppermute | solution.py:248
  213.2 29.6 %copy-start.5 = (bf16[512,512]{1,0:T(8,128)(2,1)}, bf16[512,512]{1,0:T(8,128)(2,1)S(1)}, u32[]{:S(2)}) copy-start(bf16[512,512]{1,0:T(8,128)(2,1)S(1)} %collective-permute-done.6.refs_2_) | copy-start | bytes 1572868
  213.2 13.8 %collective-permute-start.8 = (bf16[512,512]{1,0:T(8,128)(2,1)S(1)}, bf16[512,512]{1,0:T(8,128)(2,1)S(1)}, u32[]{:S(2)}, u32[]{:S(2)}) collective-permute-start(bf16[512,512]{1,0:T(8,128)(2,1)S(1)} %collective-permute-done.6.refs_2_), channel_id=1, source_target_pairs={{0,2},{1,3},{4,0},{5,1},{8,4},{9,5},{12,8},{13,9},{14,12},{15,13},... | collective-permute-start | bytes 1572872 | tf_op jit(solution)/shard_map/ppermute | solution.py:251
  219.5 23.3 %copy-start.6 = (bf16[512,512]{1,0:T(8,128)(2,1)}, bf16[512,512]{1,0:T(8,128)(2,1)S(1)}, u32[]{:S(2)}) copy-start(bf16[512,512]{1,0:T(8,128)(2,1)S(1)} %collective-permute-done.7.refs_3_) | copy-start | bytes 1572868
  219.5 12.1 %collective-permute-start.9 = (bf16[512,512]{1,0:T(8,128)(2,1)S(1)}, bf16[512,512]{1,0:T(8,128)(2,1)S(1)}, u32[]{:S(2)}, u32[]{:S(2)}) collective-permute-start(bf16[512,512]{1,0:T(8,128)(2,1)S(1)} %collective-permute-done.7.refs_3_), channel_id=1, source_target_pairs={{0,4},{1,5},{4,8},{5,9},{8,12},{9,13},{12,14},{13,15},{14,10},{15,... | collective-permute-start | bytes 1572872 | tf_op jit(solution)/shard_map/ppermute | solution.py:248
  227.1 15.7 %copy-start.7 = (bf16[512,512]{1,0:T(8,128)(2,1)}, bf16[512,512]{1,0:T(8,128)(2,1)S(1)}, u32[]{:S(2)}) copy-start(bf16[512,512]{1,0:T(8,128)(2,1)S(1)} %collective-permute-done.8.refs_4_) | copy-start | bytes 1572868
  227.1 13.0 %collective-permute-start.10 = (bf16[512,512]{1,0:T(8,128)(2,1)S(1)}, bf16[512,512]{1,0:T(8,128)(2,1)S(1)}, u32[]{:S(2)}, u32[]{:S(2)}) collective-permute-start(bf16[512,512]{1,0:T(8,128)(2,1)S(1)} %collective-permute-done.8.refs_4_), channel_id=1, source_target_pairs={{0,2},{1,3},{4,0},{5,1},{8,4},{9,5},{12,8},{13,9},{14,12},{15,13},... | collective-permute-start | bytes 1572872 | tf_op jit(solution)/shard_map/ppermute | solution.py:251
  231.6 11.3 %copy-start.8 = (bf16[512,512]{1,0:T(8,128)(2,1)}, bf16[512,512]{1,0:T(8,128)(2,1)S(1)}, u32[]{:S(2)}) copy-start(bf16[512,512]{1,0:T(8,128)(2,1)S(1)} %collective-permute-done.9.refs_5_) | copy-start | bytes 1572868
  231.6 11.2 %collective-permute-start.11 = (bf16[512,512]{1,0:T(8,128)(2,1)S(1)}, bf16[512,512]{1,0:T(8,128)(2,1)S(1)}, u32[]{:S(2)}, u32[]{:S(2)}) collective-permute-start(bf16[512,512]{1,0:T(8,128)(2,1)S(1)} %collective-permute-done.9.refs_5_), channel_id=1, source_target_pairs={{0,4},{1,5},{4,8},{5,9},{8,12},{9,13},{12,14},{13,15},{14,10},{15,... | collective-permute-start | bytes 1572872 | tf_op jit(solution)/shard_map/ppermute | solution.py:248
  259.0 47.9 %all-to-all-start.3 = ((bf16[8,256,512]{2,1,0:T(8,128)(2,1)}), bf16[8,256,512]{2,1,0:T(8,128)(2,1)S(1)}, u32[]{:S(2)}, u32[]{:S(2)}) async-start(bf16[8,256,512]{2,1,0:T(8,128)(2,1)} %bitcast.60), calls=%async_computation.3 | async-start | bytes 4194304 | tf_op jit(solution)/shard_map/all_to_all | solution.py:293
  308.2 86.3 %all-to-all-start.1 = ((bf16[8,256,512]{2,1,0:T(8,128)(2,1)}), bf16[8,256,512]{2,1,0:T(8,128)(2,1)S(1)}, u32[]{:S(2)}, u32[]{:S(2)}) async-start(bf16[8,256,512]{2,1,0:T(8,128)(2,1)} %bitcast.59), calls=%async_computation.1 | async-start | bytes 4194304 | tf_op jit(solution)/shard_map/all_to_all | solution.py:293
  326.0 39.9 %collective-permute-start.21 = (bf16[512,256]{1,0:T(8,128)(2,1)}, bf16[512,256]{1,0:T(8,128)(2,1)S(1)}, u32[]{:S(2)}, u32[]{:S(2)}) collective-permute-start(bf16[512,256]{1,0:T(8,128)(2,1)} %get-tuple-element.13.refs_2_), channel_id=1, source_target_pairs={{0,2},{1,3},{2,4},{3,5},{4,6},{5,7},{6,8},{7,9},{8,10},{9,11},{10,... | collective-permute-start | bytes 786440 | tf_op jit(solution)/shard_map/ppermute | solution.py:390
  374.4 11.4 %copy-start.29 = (s32[8192]{0:T(1024)S(1)}, s32[8192]{0:T(1024)}, u32[]{:S(2)}) copy-start(s32[8192]{0:T(1024)} %param.10) | copy-start | bytes 98308
  374.4 20.1 %collective-permute-start.23 = (bf16[512,512]{1,0:T(8,128)(2,1)}, bf16[512,512]{1,0:T(8,128)(2,1)}, u32[]{:S(2)}, u32[]{:S(2)}) collective-permute-start(bf16[512,512]{1,0:T(8,128)(2,1)} %shard_map.94), channel_id=1, source_target_pairs={{0,16},{16,0},{1,17},{17,1},{2,18},{18,2},{3,19},{19,3},{4,20},{20... | collective-permute-start | bytes 1572872 | tf_op jit(solution)/shard_map/ppermute | solution.py:290
  380.4 14.1 %collective-permute-start.17 = (bf16[512,256]{1,0:T(8,128)(2,1)}, bf16[512,256]{1,0:T(8,128)(2,1)S(1)}, u32[]{:S(2)}, u32[]{:S(2)}) collective-permute-start(bf16[512,256]{1,0:T(8,128)(2,1)} %get-tuple-element.11.refs_2_), channel_id=1, source_target_pairs={{0,2},{1,3},{2,4},{3,5},{4,6},{5,7},{6,8},{7,9},{8,10},{9,11},{10,... | collective-permute-start | bytes 786440 | tf_op jit(solution)/shard_map/ppermute | solution.py:390
  394.0 13.5 %collective-permute-start.22 = (bf16[512,512]{1,0:T(8,128)(2,1)}, bf16[512,512]{1,0:T(8,128)(2,1)S(1)}, u32[]{:S(2)}, u32[]{:S(2)}) collective-permute-start(bf16[512,512]{1,0:T(8,128)(2,1)} %shard_map.93), channel_id=1, source_target_pairs={{0,16},{16,0},{1,17},{17,1},{2,18},{18,2},{3,19},{19,3},{4,20},{20... | collective-permute-start | bytes 1572872 | tf_op jit(solution)/shard_map/ppermute | solution.py:290
  394.5 13.0 %collective-permute-start.24 = (bf16[512,512]{1,0:T(8,128)(2,1)}, bf16[512,512]{1,0:T(8,128)(2,1)S(1)}, u32[]{:S(2)}, u32[]{:S(2)}) collective-permute-start(bf16[512,512]{1,0:T(8,128)(2,1)} %collective-permute-done.23), channel_id=1, source_target_pairs={{0,1},{1,0},{2,3},{3,2},{4,5},{5,4},{6,7},{7,6},{8,9},{9,8},{10,11... | collective-permute-start | bytes 1572872 | tf_op jit(solution)/shard_map/ppermute | solution.py:287
  403.6 15.8 %collective-permute-start.18 = (bf16[512,512]{1,0:T(8,128)(2,1)}, bf16[512,512]{1,0:T(8,128)(2,1)S(1)}, u32[]{:S(2)}, u32[]{:S(2)}) collective-permute-start(bf16[512,512]{1,0:T(8,128)(2,1)} %shard_map.87), channel_id=1, source_target_pairs={{0,1},{1,0},{2,3},{3,2},{4,5},{5,4},{6,7},{7,6},{8,9},{9,8},{10,11... | collective-permute-start | bytes 1572872 | tf_op jit(solution)/shard_map/ppermute | solution.py:287
  (16 other events, 48.4 us)

commit v2 on v1

--- a/solution.py
+++ b/solution.py
@@ -13,13 +13,10 @@
 MASKED = -1e30
 QT = 128
 DP, CTX = "dp", "ctx"
-VMEM_LIMIT = 56 * 1024 * 1024
-
-
-def params(n=1):
-    return pltpu.CompilerParams(
-        dimension_semantics=("arbitrary",) * n, vmem_limit_bytes=VMEM_LIMIT
-    )
+
+
+def params(mib=24):
+    return pltpu.CompilerParams(vmem_limit_bytes=mib * 1024 * 1024)
 
 
 def project_kernel(koff, x, slots, *refs):
@@ -74,7 +71,7 @@
         grid_spec=grid_spec,
         out_shape=jax.ShapeDtypeStruct((chips, 2, per, n), x.dtype),
         input_output_aliases={3 + chips: 0} if more else {},
-        compiler_params=params(),
+        compiler_params=params(60),
     )(koff, x, slots, *ws, *more)
 
 
@@ -129,15 +126,16 @@
     span = rows + QT
     v = unpack_rows(got[...].reshape(-1, got.shape[-1]), target[0], rows)
     for h in range(heads):
-        q[h] = rotated(v[:, h * HEAD : (h + 1) * HEAD], cosine[...], sine[...]).astype(q.dtype)
+        turned = rotated(v[:, h * HEAD : (h + 1) * HEAD], cosine[...], sine[...])
+        q[h] = (turned * HEAD**-0.5).astype(q.dtype)
     for e in range(2):
 
         @pl.when(d ^ core[0] == e)
         def _(e=e):
-            kv[:rows] = blocks[e][...]
-            kv[rows:] = blocks[e + 1][...]
-
-    scale = HEAD**-0.5
+            kv[:rows, : 2 * HEAD] = blocks[e][...]
+            kv[rows:, : 2 * HEAD] = blocks[e + 1][...]
+
+    kv[:, 2 * HEAD :] = jnp.ones((2 * rows, HEAD), kv.dtype)
 
     def tile(i, carry):
         at = pl.multiple_of(i * QT, QT)
@@ -154,13 +152,11 @@
             qdocs[pl.ds(at, QT), :1] == kdocs[0, :, pl.ds(at, span)]
         )
         s = jnp.where(ok[None], s, MASKED)
-        top = jnp.max(s, axis=-1, keepdims=True)
-        w = jnp.exp((s - top) * scale)
-        total = jnp.sum(w, axis=-1, keepdims=True)
+        w = jnp.exp(s - jnp.max(s, axis=-1, keepdims=True))
         o = jnp.dot(
             w.astype(kv.dtype).reshape(heads * QT, span), vs, preferred_element_type=jnp.float32
-        ).reshape(heads, QT, HEAD)
-        o = o / total
+        ).reshape(heads, QT, 2 * HEAD)
+        o = o[..., :HEAD] / o[..., HEAD:]
         for h in range(heads):
             out[pl.ds(at, QT), h * HEAD : (h + 1) * HEAD] = o[h].astype(out.dtype)
         return carry
@@ -186,7 +182,7 @@
         out_specs=pl.BlockSpec((rows, n), lambda i, s: (0, s[1] if more else 0)),
         scratch_shapes=[
             pltpu.VMEM((n // HEAD, rows, HEAD), got.dtype),
-            pltpu.VMEM((2 * rows, 2 * HEAD), got.dtype),
+            pltpu.VMEM((2 * rows, 3 * HEAD), got.dtype),
         ],
     )
     shape = base.shape if more else (rows, n)

time: 424 us -> 417 us (0.983)
  Pallas kernels: 96.1 us -> 83.8 us
    unnamed x68 -> x84, local copies, waits for them, and re-layouts: 5.61 us -> 13.3 us
    pallas_call x4, Pallas kernels: 30 us -> 22.3 us  [attend(): pl.pallas_call(functools.partial(attend_kernel, d), grid_spec=grid_spec,...]
  transfers between devices with their start and end apart: 30 -> 30, of which waited for: 18 -> 19; matrix products, arithmetic and copies ran while one was open for 4% -> 3% of each run, Pallas kernels for 22% -> 20%
where the time goes in v2:
time: 417 us; the launch traced here: 416 us
  waiting for transfers between devices  247 us (59%)
  Pallas kernels  83.8 us (20%)
  starting transfers between devices  59.2 us (14%)
  local copies, waits for them, and re-layouts  18.9 us (5%)
  other arithmetic  6.53 us (2%)
    ppermute x4, waiting for transfers between devices, to_side(): return lax.ppermute(x, DP, side_pairs)  95.3 us
    pallas_call x8, Pallas kernels, project(): pl.pallas_call(project_kernel, grid_spec=grid_spec, out_shape=jax.ShapeDt...  53.2 us
    ppermute x2, waiting for transfers between devices, keys_of(): return (lax.ppermute(second, CTX, ahead), first, second)  38.6 us
    ppermute x6, waiting for transfers between devices, ring_gather(): b = lax.ppermute(b, CTX, back)  38.3 us
    all_to_all x4, waiting for transfers between devices, exchange(): lax.all_to_all(x, CTX, split_axis=0, concat_axis=0, tiled=True, axis_inde...  37.4 us
    ppermute x8, waiting for transfers between devices, ring_gather(): a = lax.ppermute(a, CTX, forth)  31.4 us
    all_to_all x4, starting transfers between devices, exchange(): lax.all_to_all(x, CTX, split_axis=0, concat_axis=0, tiled=True, axis_inde...  23.5 us
    pallas_call x4, Pallas kernels, attend(): pl.pallas_call(functools.partial(attend_kernel, d), grid_spec=grid_spec,...  22.3 us
  transfers between devices with their start and end apart: 30, of which 19 were waited for; matrix products, arithmetic and copies ran while one was open for 3% of the time, Pallas kernels for 20%

profile of v2, /device:TPU:12, one launch (start us, length us, event | category | flops | bytes accessed | tf_op | source)
XLA Modules:
  0.0 416.2 jit_solution(7655135632707221949)
XLA Ops:
  0.0 1.6 collective-permute-start.19
  2.6 90.1 %collective-permute-done.19.x = bf16[512,4096]{1,0:T(8,128)(2,1)} collective-permute-done((bf16[512,4096]{1,0:T(8,128)(2,1)}, bf16[512,4096]{1,0:T(8,128)(2,1)}, u32[]{:S(2)}, u32[]{:S(2)}) %collective-permute-start.19) | collective-permute-done | bytes 4194336 | tf_op jit(solution)/shard_map/ppermute | solution.py:286
  94.3 1.6 collective-permute-start.1
  96.5 4.1 collective-permute-done.2
  100.7 1.6 collective-permute-start.3
  104.8 6.2 %all-to-all-start = ((s32[16,2,512]{2,1,0:T(2,128)}), s32[16,2,512]{2,1,0:T(2,128)S(1)}, u32[]{:S(2)}, u32[]{:S(2)}) async-start(s32[16,2,512]{2,1,0:T(2,128)} %broadcast_in_dim.34), calls=%async_computation | async-start | bytes 131072 | tf_op jit(solution)/shard_map/all_to_all | solution.py:321
  113.9 1.6 all-to-all-done
  115.5 4.0 collective-permute-done.4.refs_4_
  119.5 1.6 collective-permute-done.13.refs_3_
  124.6 4.0 collective-permute-done.14.refs_5_
  130.4 5.0 %collective-permute-done.16.refs_7_ = bf16[512,256]{1,0:T(8,128)(2,1)S(1)} collective-permute-done((bf16[512,256]{1,0:T(8,128)(2,1)S(1)}, bf16[512,256]{1,0:T(8,128)(2,1)S(1)}, u32[]{:S(2)}, u32[]{:S(2)}) %collective-permute-start.16) | collective-permute-done | bytes 262176 | tf_op jit(solution)/shard_map/ppermute | solution.py:244
  136.0 5.6 %shard_map.84.refs_8_ = bf16[8,2,128,256]{3,2,1,0:T(8,128)(2,1)} custom-call(s32[16]{0:T(128)} %mul.90.koff, bf16[512,4096]{1,0:T(8,128)(2,1)} %x.7, s32[2,1,512]{2,1,0:T(1,128)} %get-tuple-element.30.slots, bf16[512,256]{1,0:T(8,128)(2,1)} %copy-done.23, bf16[512,256]{1,0:T(8,128)(2,1)} %copy-done.25, bf16[512,256]{1,0:T(8,128)(2,1)} %copy-done.24, ...), custom_call_target="tpu_custom_call" | custom-call | tf_op jit(solution)/shard_map/pallas_call | solution.py:69
  141.6 5.6 %shard_map.85 = bf16[8,2,128,256]{3,2,1,0:T(8,128)(2,1)} custom-call(s32[16]{0:T(128)} %mul.90.koff, bf16[512,4096]{1,0:T(8,128)(2,1)} %collective-permute-done.x, s32[2,1,512]{2,1,0:T(1,128)} %get-tuple-element.30.slots, bf16[512,256]{1,0:T(8,128)(2,1)} %copy-done.23, bf16[512,256]{1,0:T(8,128)(2,1)} %copy-done.25, ...), custom_call_target="tpu_custom_call", output_to_operand_aliasing={{}: (11, {})} | custom-call | tf_op jit(solution)/shard_map/pallas_call | solution.py:69
  147.2 5.0 %all-to-all-start.2 = ((bf16[8,256,256]{2,1,0:T(8,128)(2,1)}), bf16[8,256,256]{2,1,0:T(8,128)(2,1)S(1)}, u32[]{:S(2)}, u32[]{:S(2)}) async-start(bf16[8,256,256]{2,1,0:T(8,128)(2,1)} %bitcast.64), calls=%async_computation.2 | async-start | bytes 2097152 | tf_op jit(solution)/shard_map/all_to_all | solution.py:289
  152.9 5.6 %shard_map.90.refs_8_ = bf16[8,2,128,256]{3,2,1,0:T(8,128)(2,1)} custom-call(s32[16]{0:T(128)} %mul.90.koff, bf16[512,4096]{1,0:T(8,128)(2,1)} %collective-permute-done.19.x, s32[2,1,512]{2,1,0:T(1,128)} %get-tuple-element.29.slots, bf16[512,256]{1,0:T(8,128)(2,1)} %copy-done.23, bf16[512,256]{1,0:T(8,128)(2,1)} %copy-done.25, bf16[512,256]{1,0:T(8,128)(2,1)} %copy-done.24, ...), custom_call_target="tpu_custom_call" | custom-call | tf_op jit(solution)/shard_map/pallas_call | solution.py:69
  158.5 5.6 %shard_map.91 = bf16[8,2,128,256]{3,2,1,0:T(8,128)(2,1)} custom-call(s32[16]{0:T(128)} %mul.90.koff, bf16[512,4096]{1,0:T(8,128)(2,1)} %collective-permute-done.20.x, s32[2,1,512]{2,1,0:T(1,128)} %get-tuple-element.29.slots, bf16[512,256]{1,0:T(8,128)(2,1)} %copy-done.23, bf16[512,256]{1,0:T(8,128)(2,1)} %copy-done.25, ...), custom_call_target="tpu_custom_call", output_to_operand_aliasing={{}: (11, {})} | custom-call | tf_op jit(solution)/shard_map/pallas_call | solution.py:69
  164.1 9.2 %all-to-all-done.2 = bf16[8,256,256]{2,1,0:T(8,128)(2,1)S(1)} async-done(((bf16[8,256,256]{2,1,0:T(8,128)(2,1)}), bf16[8,256,256]{2,1,0:T(8,128)(2,1)S(1)}, u32[]{:S(2)}, u32[]{:S(2)}) %all-to-all-start.2) | async-done | bytes 1048608 | tf_op jit(solution)/shard_map/all_to_all | solution.py:289
  173.2 7.4 %all-to-all-start.4 = ((bf16[8,256,256]{2,1,0:T(8,128)(2,1)}), bf16[8,256,256]{2,1,0:T(8,128)(2,1)S(1)}, u32[]{:S(2)}, u32[]{:S(2)}) async-start(bf16[8,256,256]{2,1,0:T(8,128)(2,1)} %bitcast.63), calls=%async_computation.4 | async-start | bytes 2097152 | tf_op jit(solution)/shard_map/all_to_all | solution.py:289
  182.1 13.1 %collective-permute-done.5.refs_1_ = bf16[512,512]{1,0:T(8,128)(2,1)S(1)} collective-permute-done((bf16[512,512]{1,0:T(8,128)(2,1)S(1)}, bf16[512,512]{1,0:T(8,128)(2,1)S(1)}, u32[]{:S(2)}, u32[]{:S(2)}) %collective-permute-start.5) | collective-permute-done | bytes 524320 | tf_op jit(solution)/shard_map/ppermute | solution.py:244
  195.3 18.1 %collective-permute-done.6.refs_2_ = bf16[512,512]{1,0:T(8,128)(2,1)S(1)} collective-permute-done((bf16[512,512]{1,0:T(8,128)(2,1)S(1)}, bf16[512,512]{1,0:T(8,128)(2,1)S(1)}, u32[]{:S(2)}, u32[]{:S(2)}) %collective-permute-start.6) | collective-permute-done | bytes 524320 | tf_op jit(solution)/shard_map/ppermute | solution.py:247
  213.4 2.5 collective-permute-start.8
  215.8 3.7 collective-permute-done.7.refs_3_
  219.6 7.6 %collective-permute-done.8.refs_4_ = bf16[512,512]{1,0:T(8,128)(2,1)S(1)} collective-permute-done((bf16[512,512]{1,0:T(8,128)(2,1)S(1)}, bf16[512,512]{1,0:T(8,128)(2,1)S(1)}, u32[]{:S(2)}, u32[]{:S(2)}) %collective-permute-start.8) | collective-permute-done | bytes 524320 | tf_op jit(solution)/shard_map/ppermute | solution.py:247
  227.2 2.5 collective-permute-start.10
  229.7 2.0 collective-permute-done.9.refs_5_
  232.0 8.2 %collective-permute-done.10.refs_6_ = bf16[512,512]{1,0:T(8,128)(2,1)S(1)} collective-permute-done((bf16[512,512]{1,0:T(8,128)(2,1)S(1)}, bf16[512,512]{1,0:T(8,128)(2,1)S(1)}, u32[]{:S(2)}, u32[]{:S(2)}) %collective-permute-start.10) | collective-permute-done | bytes 524320 | tf_op jit(solution)/shard_map/ppermute | solution.py:247
  241.0 2.1 collective-permute-done.11.refs_7_
  243.1 7.7 %shard_map.88.refs_8_ = bf16[8,2,128,512]{3,2,1,0:T(8,128)(2,1)} custom-call(s32[16]{0:T(128)} %mul.90.koff, bf16[512,4096]{1,0:T(8,128)(2,1)} %collective-permute-done.19.x, s32[2,1,512]{2,1,0:T(1,128)} %get-tuple-element.29.slots, bf16[512,512]{1,0:T(8,128)(2,1)} %copy-done.16, bf16[512,512]{1,0:T(8,128)(2,1)} %copy-done.17, bf16[512,512]{1,0:T(8,128)(2,1)} %copy-done.18, ...), custom_call_target="tpu_custom_call" | custom-call | tf_op jit(solution)/shard_map/pallas_call | solution.py:69
  250.8 7.7 %shard_map.89 = bf16[8,2,128,512]{3,2,1,0:T(8,128)(2,1)} custom-call(s32[16]{0:T(128)} %mul.90.koff, bf16[512,4096]{1,0:T(8,128)(2,1)} %collective-permute-done.20.x, s32[2,1,512]{2,1,0:T(1,128)} %get-tuple-element.29.slots, bf16[512,512]{1,0:T(8,128)(2,1)} %copy-done.16, bf16[512,512]{1,0:T(8,128)(2,1)} %copy-done.17, ...), custom_call_target="tpu_custom_call", output_to_operand_aliasing={{}: (11, {})} | custom-call | tf_op jit(solution)/shard_map/pallas_call | solution.py:69
  259.5 4.2 %all-to-all-start.3 = ((bf16[8,256,512]{2,1,0:T(8,128)(2,1)}), bf16[8,256,512]{2,1,0:T(8,128)(2,1)S(1)}, u32[]{:S(2)}, u32[]{:S(2)}) async-start(bf16[8,256,512]{2,1,0:T(8,128)(2,1)} %bitcast.62), calls=%async_computation.3 | async-start | bytes 4194304 | tf_op jit(solution)/shard_map/all_to_all | solution.py:289
  263.7 7.7 %shard_map.82.refs_8_ = bf16[8,2,128,512]{3,2,1,0:T(8,128)(2,1)} custom-call(s32[16]{0:T(128)} %mul.90.koff, bf16[512,4096]{1,0:T(8,128)(2,1)} %x.7, s32[2,1,512]{2,1,0:T(1,128)} %get-tuple-element.30.slots, bf16[512,512]{1,0:T(8,128)(2,1)} %copy-done.16, bf16[512,512]{1,0:T(8,128)(2,1)} %copy-done.17, bf16[512,512]{1,0:T(8,128)(2,1)} %copy-done.18, ...), custom_call_target="tpu_custom_call" | custom-call | tf_op jit(solution)/shard_map/pallas_call | solution.py:69
  271.4 7.7 %shard_map.83 = bf16[8,2,128,512]{3,2,1,0:T(8,128)(2,1)} custom-call(s32[16]{0:T(128)} %mul.90.koff, bf16[512,4096]{1,0:T(8,128)(2,1)} %collective-permute-done.x, s32[2,1,512]{2,1,0:T(1,128)} %get-tuple-element.30.slots, bf16[512,512]{1,0:T(8,128)(2,1)} %copy-done.16, bf16[512,512]{1,0:T(8,128)(2,1)} %copy-done.17, ...), custom_call_target="tpu_custom_call", output_to_operand_aliasing={{}: (11, {})} | custom-call | tf_op jit(solution)/shard_map/pallas_call | solution.py:69
  279.2 28.2 %all-to-all-done.3 = bf16[8,256,512]{2,1,0:T(8,128)(2,1)S(1)} async-done(((bf16[8,256,512]{2,1,0:T(8,128)(2,1)}), bf16[8,256,512]{2,1,0:T(8,128)(2,1)S(1)}, u32[]{:S(2)}, u32[]{:S(2)}) %all-to-all-start.3) | async-done | bytes 2097184 | tf_op jit(solution)/shard_map/all_to_all | solution.py:289
  308.7 6.9 %all-to-all-start.1 = ((bf16[8,256,512]{2,1,0:T(8,128)(2,1)}), bf16[8,256,512]{2,1,0:T(8,128)(2,1)S(1)}, u32[]{:S(2)}, u32[]{:S(2)}) async-start(bf16[8,256,512]{2,1,0:T(8,128)(2,1)} %bitcast.61), calls=%async_computation.1 | async-start | bytes 4194304 | tf_op jit(solution)/shard_map/all_to_all | solution.py:289
  315.7 1.9 fusion.7
  318.6 1.9 select_reduce_fusion
  321.8 2.5 shard_map.92
  324.3 3.4 collective-permute-start.21
  327.8 38.6 %collective-permute-done.21.refs_0_ = bf16[512,256]{1,0:T(8,128)(2,1)} collective-permute-done((bf16[512,256]{1,0:T(8,128)(2,1)}, bf16[512,256]{1,0:T(8,128)(2,1)}, u32[]{:S(2)}, u32[]{:S(2)}) %collective-permute-start.21) | collective-permute-done | bytes 262176 | tf_op jit(solution)/shard_map/ppermute | solution.py:386
  366.6 1.6 copy-done.1
  368.2 6.3 %shard_map.94 = bf16[512,512]{1,0:T(8,128)(2,1)} custom-call(s32[2]{0:T(128)S(1)} %pad_add_fusion.4.core.scalars, bf16[8,2,2,64,512]{4,3,2,1,0:T(8,128)(2,1)S(1)} %bitcast.57, s32[2,1,1024]{2,1,0:T(1,128)S(1)} %squeeze.30.target, bf16[512,256]{1,0:T(8,128)(2,1)} %collective-permute-done.21.refs_0_, bf16[512,256]{1,0:T(8,128)(2,1)S(1)} %get-tuple-element.14.refs_1_, ...), custom_call_target="tpu_custom_call" | custom-call | tf_op jit(solution)/shard_map/pallas_call | solution.py:189
  377.5 1.8 shard_map.86
  379.2 5.5 %collective-permute-start.17 = (bf16[512,256]{1,0:T(8,128)(2,1)S(1)}, bf16[512,256]{1,0:T(8,128)(2,1)S(1)}, u32[]{:S(2)}, u32[]{:S(2)}) collective-permute-start(bf16[512,256]{1,0:T(8,128)(2,1)S(1)} %get-tuple-element.11.refs_2_), channel_id=1, source_target_pairs={{0,2},{1,3},{2,4},{3,5},{4,6},{5,7},{6,8},{7,9},{8,10},{9,11},{10,... | collective-permute-start | bytes 786440 | tf_op jit(solution)/shard_map/ppermute | solution.py:386
  386.9 6.3 %shard_map.93 = bf16[512,512]{1,0:T(8,128)(2,1)} custom-call(s32[2]{0:T(128)S(1)} %pad_add_fusion.4.core.scalars, bf16[8,2,2,64,512]{4,3,2,1,0:T(8,128)(2,1)S(1)} %bitcast.58, s32[2,1,1024]{2,1,0:T(1,128)S(1)} %squeeze.30.target, bf16[512,256]{1,0:T(8,128)(2,1)} %collective-permute-done.21.refs_0_, bf16[512,256]{1,0:T(8,128)(2,1)S(1)} %copy-done.14, ...), custom_call_target="tpu_custom_call" | custom-call | tf_op jit(solution)/shard_map/pallas_call | solution.py:189
  396.6 4.4 %shard_map.87 = bf16[512,512]{1,0:T(8,128)(2,1)S(1)} custom-call(s32[2]{0:T(128)S(1)} %pad_add_fusion.4.core.scalars, bf16[8,2,2,64,512]{4,3,2,1,0:T(8,128)(2,1)S(1)} %bitcast.55, s32[2,1,1024]{2,1,0:T(1,128)S(1)} %squeeze.14.target, bf16[512,256]{1,0:T(8,128)(2,1)S(1)} %copy-done.12, bf16[512,256]{1,0:T(8,128)(2,1)S(1)} %get-tuple-element.12.refs_1_, ...), custom_call_target="tpu_custom_call" | custom-call | tf_op jit(solution)/shard_map/pallas_call | solution.py:189
  401.6 5.2 %collective-permute-done.22.refs_0_ = bf16[512,512]{1,0:T(8,128)(2,1)} collective-permute-done((bf16[512,512]{1,0:T(8,128)(2,1)}, bf16[512,512]{1,0:T(8,128)(2,1)}, u32[]{:S(2)}, u32[]{:S(2)}) %collective-permute-start.22) | collective-permute-done | bytes 524320 | tf_op jit(solution)/shard_map/ppermute | solution.py:286
  406.8 2.8 shard_map.95.refs_7_
  409.6 5.2 %shard_map.96.refs_1_ = bf16[512,2048]{1,0:T(8,128)(2,1)} custom-call(s32[2]{0:T(128)S(1)} %pad_add_fusion.4.core.scalars, bf16[8,2,2,64,512]{4,3,2,1,0:T(8,128)(2,1)S(1)} %bitcast.56, s32[2,1,1024]{2,1,0:T(1,128)S(1)} %squeeze.14.target, bf16[512,256]{1,0:T(8,128)(2,1)S(1)} %copy-done.12, ...), custom_call_target="tpu_custom_call", output_to_operand_aliasing={{}: (10, {})} | custom-call | tf_op jit(solution)/shard_map/pallas_call | solution.py:189
  (161 shorter events, 33.1 us)
Async XLA Ops:
  0.0 95.9 %copy-start.15 = (s32[8]{0:T(128)S(1)}, s32[8]{0:T(128)}, u32[]{:S(2)}) copy-start(s32[8]{0:T(128)} %constant.131.clone) | copy-start | bytes 100
  0.0 102.8 %copy-start.41 = (s32[8]{0:T(128)S(1)}, s32[8]{0:T(128)}, u32[]{:S(2)}) copy-start(s32[8]{0:T(128)} %constant.132.clone) | copy-start | bytes 100
  0.0 94.3 %copy-start.36 = (s32[8192]{0:T(1024)S(1)}, s32[8192]{0:T(1024)}, u32[]{:S(2)}) copy-start(s32[8192]{0:T(1024)} %param.10) | copy-start | bytes 98308
  0.0 94.3 %copy-start.40 = (s32[512]{0:T(512)S(1)}, s32[512]{0:T(512)}, u32[]{:S(2)}) copy-start(s32[512]{0:T(512)} %param.9) | copy-start | bytes 6148
  0.0 92.7 %collective-permute-start.19 = (bf16[512,4096]{1,0:T(8,128)(2,1)}, bf16[512,4096]{1,0:T(8,128)(2,1)}, u32[]{:S(2)}, u32[]{:S(2)}) collective-permute-start(bf16[512,4096]{1,0:T(8,128)(2,1)} %x.7), channel_id=1, source_target_pairs={{0,16},{16,0},{1,17},{17,1},{2,18},{18,2},{3,19},{19,3},{4,20},{20... | collective-permute-start | bytes 12582920 | tf_op jit(solution)/shard_map/ppermute | solution.py:286
  1.6 140.0 %collective-permute-start = (bf16[512,4096]{1,0:T(8,128)(2,1)}, bf16[512,4096]{1,0:T(8,128)(2,1)}, u32[]{:S(2)}, u32[]{:S(2)}) collective-permute-start(bf16[512,4096]{1,0:T(8,128)(2,1)} %x.7), channel_id=1, source_target_pairs={{0,1},{1,0},{2,3},{3,2},{4,5},{5,4},{6,7},{7,6},{8,9},{9,8},{10,11... | collective-permute-start | bytes 12582920 | tf_op jit(solution)/shard_map/ppermute | solution.py:283
  92.7 65.8 %collective-permute-start.20 = (bf16[512,4096]{1,0:T(8,128)(2,1)}, bf16[512,4096]{1,0:T(8,128)(2,1)}, u32[]{:S(2)}, u32[]{:S(2)}) collective-permute-start(bf16[512,4096]{1,0:T(8,128)(2,1)} %collective-permute-done.19.x), channel_id=1, source_target_pairs={{0,1},{1,0},{2,3},{3,2},{4,5},{5,4},{6,7},{7,6},{8,9},{9,8},{10,11... | collective-permute-start | bytes 12582920 | tf_op jit(solution)/shard_map/ppermute | solution.py:283
  93.7 6.9 %collective-permute-start.2 = (bf16[256,768]{1,0:T(8,128)(2,1)S(1)}, bf16[256,768]{1,0:T(8,128)(2,1)S(1)}, u32[]{:S(2)}, u32[]{:S(2)}) collective-permute-start(bf16[256,768]{1,0:T(8,128)(2,1)S(1)} %pad_maximum_fusion.5), channel_id=1, source_target_pairs={{0,1},{1,0},{2,3},{3,2},{4,5},{5,4},{6,7},{7,6},{8,9},{9,8},{10,11... | collective-permute-start | bytes 1179656 | tf_op jit(solution)/shard_map/ppermute | solution.py:283
  94.3 9.8 %collective-permute-start.1 = (s32[8704]{0:T(1024)S(1)}, s32[8704]{0:T(1024)S(1)}, u32[]{:S(2)}, u32[]{:S(2)}) collective-permute-start(s32[8704]{0:T(1024)S(1)} %pad_add_fusion), channel_id=1, source_target_pairs={{0,16},{16,0},{1,17},{17,1},{2,18},{18,2},{3,19},{19,3},{4,20},{20... | collective-permute-start | bytes 104456 | tf_op jit(solution)/shard_map/ppermute | solution.py:286
  100.6 41.0 %copy-start.31 = (bf16[256,768]{1,0:T(8,128)(2,1)}, bf16[256,768]{1,0:T(8,128)(2,1)S(1)}, u32[]{:S(2)}) copy-start(bf16[256,768]{1,0:T(8,128)(2,1)S(1)} %collective-permute-done.2) | copy-start | bytes 1179652
  100.7 34.7 %copy-start.23 = (bf16[512,256]{1,0:T(8,128)(2,1)}, bf16[512,256]{1,0:T(8,128)(2,1)S(1)}, u32[]{:S(2)}) copy-start(bf16[512,256]{1,0:T(8,128)(2,1)S(1)} %pad_maximum_fusion.6.refs_0_) | copy-start | bytes 786436
  100.7 10.3 %collective-permute-start.3 = (bf16[512,256]{1,0:T(8,128)(2,1)S(1)}, bf16[512,256]{1,0:T(8,128)(2,1)S(1)}, u32[]{:S(2)}, u32[]{:S(2)}) collective-permute-start(bf16[512,256]{1,0:T(8,128)(2,1)S(1)} %pad_maximum_fusion.6.refs_0_), channel_id=1, source_target_pairs={{0,2},{1,3},{4,0},{5,1},{8,4},{9,5},{12,8},{13,9},{14,12},{15,13},... | collective-permute-start | bytes 786440 | tf_op jit(solution)/shard_map/ppermute | solution.py:247
  102.3 10.2 %collective-permute-start.12 = (bf16[512,256]{1,0:T(8,128)(2,1)S(1)}, bf16[512,256]{1,0:T(8,128)(2,1)S(1)}, u32[]{:S(2)}, u32[]{:S(2)}) collective-permute-start(bf16[512,256]{1,0:T(8,128)(2,1)S(1)} %pad_maximum_fusion.6.refs_0_), channel_id=1, source_target_pairs={{0,4},{1,5},{4,8},{5,9},{8,12},{9,13},{12,14},{13,15},{14,10},{15,... | collective-permute-start | bytes 786440 | tf_op jit(solution)/shard_map/ppermute | solution.py:244
  104.8 10.7 %all-to-all-start = ((s32[16,2,512]{2,1,0:T(2,128)}), s32[16,2,512]{2,1,0:T(2,128)S(1)}, u32[]{:S(2)}, u32[]{:S(2)}) async-start(s32[16,2,512]{2,1,0:T(2,128)} %broadcast_in_dim.34), calls=%async_computation | async-start | bytes 131072 | tf_op jit(solution)/shard_map/all_to_all | solution.py:321
  111.0 24.3 %copy-start.24 = (bf16[512,256]{1,0:T(8,128)(2,1)}, bf16[512,256]{1,0:T(8,128)(2,1)S(1)}, u32[]{:S(2)}) copy-start(bf16[512,256]{1,0:T(8,128)(2,1)S(1)} %collective-permute-done.3.refs_2_) | copy-start | bytes 786436
  111.0 8.4 %collective-permute-start.4 = (bf16[512,256]{1,0:T(8,128)(2,1)S(1)}, bf16[512,256]{1,0:T(8,128)(2,1)S(1)}, u32[]{:S(2)}, u32[]{:S(2)}) collective-permute-start(bf16[512,256]{1,0:T(8,128)(2,1)S(1)} %collective-permute-done.3.refs_2_), channel_id=1, source_target_pairs={{0,2},{1,3},{4,0},{5,1},{8,4},{9,5},{12,8},{13,9},{14,12},{15,13},... | collective-permute-start | bytes 786440 | tf_op jit(solution)/shard_map/ppermute | solution.py:247
  112.6 22.8 %copy-start.25 = (bf16[512,256]{1,0:T(8,128)(2,1)}, bf16[512,256]{1,0:T(8,128)(2,1)S(1)}, u32[]{:S(2)}) copy-start(bf16[512,256]{1,0:T(8,128)(2,1)S(1)} %collective-permute-done.12.refs_1_) | copy-start | bytes 786436
  112.6 8.5 %collective-permute-start.13 = (bf16[512,256]{1,0:T(8,128)(2,1)S(1)}, bf16[512,256]{1,0:T(8,128)(2,1)S(1)}, u32[]{:S(2)}, u32[]{:S(2)}) collective-permute-start(bf16[512,256]{1,0:T(8,128)(2,1)S(1)} %collective-permute-done.12.refs_1_), channel_id=1, source_target_pairs={{0,4},{1,5},{4,8},{5,9},{8,12},{9,13},{12,14},{13,15},{14,10},{15,... | collective-permute-start | bytes 786440 | tf_op jit(solution)/shard_map/ppermute | solution.py:244
  119.5 15.9 %copy-start.26 = (bf16[512,256]{1,0:T(8,128)(2,1)}, bf16[512,256]{1,0:T(8,128)(2,1)S(1)}, u32[]{:S(2)}) copy-start(bf16[512,256]{1,0:T(8,128)(2,1)S(1)} %collective-permute-done.4.refs_4_) | copy-start | bytes 786436
  121.0 14.3 %copy-start.27 = (bf16[512,256]{1,0:T(8,128)(2,1)}, bf16[512,256]{1,0:T(8,128)(2,1)S(1)}, u32[]{:S(2)}) copy-start(bf16[512,256]{1,0:T(8,128)(2,1)S(1)} %collective-permute-done.13.refs_3_) | copy-start | bytes 786436
  121.0 7.6 %collective-permute-start.14 = (bf16[512,256]{1,0:T(8,128)(2,1)S(1)}, bf16[512,256]{1,0:T(8,128)(2,1)S(1)}, u32[]{:S(2)}, u32[]{:S(2)}) collective-permute-start(bf16[512,256]{1,0:T(8,128)(2,1)S(1)} %collective-permute-done.13.refs_3_), channel_id=1, source_target_pairs={{0,4},{1,5},{4,8},{5,9},{8,12},{9,13},{12,14},{13,15},{14,10},{15,... | collective-permute-start | bytes 786440 | tf_op jit(solution)/shard_map/ppermute | solution.py:244
  123.1 7.3 %collective-permute-start.15 = (bf16[512,256]{1,0:T(8,128)(2,1)S(1)}, bf16[512,256]{1,0:T(8,128)(2,1)S(1)}, u32[]{:S(2)}, u32[]{:S(2)}) collective-permute-start(bf16[512,256]{1,0:T(8,128)(2,1)S(1)} %collective-permute-done.4.refs_4_), channel_id=1, source_target_pairs={{0,2},{1,3},{4,0},{5,1},{8,4},{9,5},{12,8},{13,9},{14,12},{15,13},... | collective-permute-start | bytes 786440 | tf_op jit(solution)/shard_map/ppermute | solution.py:247
  128.6 6.7 %collective-permute-start.16 = (bf16[512,256]{1,0:T(8,128)(2,1)S(1)}, bf16[512,256]{1,0:T(8,128)(2,1)S(1)}, u32[]{:S(2)}, u32[]{:S(2)}) collective-permute-start(bf16[512,256]{1,0:T(8,128)(2,1)S(1)} %collective-permute-done.14.refs_5_), channel_id=1, source_target_pairs={{0,4},{1,5},{4,8},{5,9},{8,12},{9,13},{12,14},{13,15},{14,10},{15,... | collective-permute-start | bytes 786440 | tf_op jit(solution)/shard_map/ppermute | solution.py:244
  147.2 26.1 %all-to-all-start.2 = ((bf16[8,256,256]{2,1,0:T(8,128)(2,1)}), bf16[8,256,256]{2,1,0:T(8,128)(2,1)S(1)}, u32[]{:S(2)}, u32[]{:S(2)}) async-start(bf16[8,256,256]{2,1,0:T(8,128)(2,1)} %bitcast.64), calls=%async_computation.2 | async-start | bytes 2097152 | tf_op jit(solution)/shard_map/all_to_all | solution.py:289
  152.2 28.4 %copy-start.16 = (bf16[512,512]{1,0:T(8,128)(2,1)}, bf16[512,512]{1,0:T(8,128)(2,1)S(1)}, u32[]{:S(2)}) copy-start(bf16[512,512]{1,0:T(8,128)(2,1)S(1)} %pad_maximum_fusion.refs_0_) | copy-start | bytes 1572868
  152.3 43.0 %collective-permute-start.5 = (bf16[512,512]{1,0:T(8,128)(2,1)S(1)}, bf16[512,512]{1,0:T(8,128)(2,1)S(1)}, u32[]{:S(2)}, u32[]{:S(2)}) collective-permute-start(bf16[512,512]{1,0:T(8,128)(2,1)S(1)} %pad_maximum_fusion.refs_0_), channel_id=1, source_target_pairs={{0,4},{1,5},{4,8},{5,9},{8,12},{9,13},{12,14},{13,15},{14,10},{15,... | collective-permute-start | bytes 1572872 | tf_op jit(solution)/shard_map/ppermute | solution.py:244
  173.2 77.5 %copy-start.5 = (bf16[8,256,256]{2,1,0:T(8,128)(2,1)}, bf16[8,256,256]{2,1,0:T(8,128)(2,1)S(1)}, u32[]{:S(2)}) copy-start(bf16[8,256,256]{2,1,0:T(8,128)(2,1)S(1)} %all-to-all-done.2) | copy-start | bytes 3145732
  173.2 85.3 %all-to-all-start.4 = ((bf16[8,256,256]{2,1,0:T(8,128)(2,1)}), bf16[8,256,256]{2,1,0:T(8,128)(2,1)S(1)}, u32[]{:S(2)}, u32[]{:S(2)}) async-start(bf16[8,256,256]{2,1,0:T(8,128)(2,1)} %bitcast.63), calls=%async_computation.4 | async-start | bytes 2097152 | tf_op jit(solution)/shard_map/all_to_all | solution.py:289
  180.7 32.7 %collective-permute-start.6 = (bf16[512,512]{1,0:T(8,128)(2,1)S(1)}, bf16[512,512]{1,0:T(8,128)(2,1)S(1)}, u32[]{:S(2)}, u32[]{:S(2)}) collective-permute-start(bf16[512,512]{1,0:T(8,128)(2,1)S(1)} %pad_maximum_fusion.refs_0_), channel_id=1, source_target_pairs={{0,2},{1,3},{4,0},{5,1},{8,4},{9,5},{12,8},{13,9},{14,12},{15,13},... | collective-permute-start | bytes 1572872 | tf_op jit(solution)/shard_map/ppermute | solution.py:247
  195.3 47.8 %copy-start.17 = (bf16[512,512]{1,0:T(8,128)(2,1)}, bf16[512,512]{1,0:T(8,128)(2,1)S(1)}, u32[]{:S(2)}) copy-start(bf16[512,512]{1,0:T(8,128)(2,1)S(1)} %collective-permute-done.5.refs_1_) | copy-start | bytes 1572868
  195.3 24.3 %collective-permute-start.7 = (bf16[512,512]{1,0:T(8,128)(2,1)S(1)}, bf16[512,512]{1,0:T(8,128)(2,1)S(1)}, u32[]{:S(2)}, u32[]{:S(2)}) collective-permute-start(bf16[512,512]{1,0:T(8,128)(2,1)S(1)} %collective-permute-done.5.refs_1_), channel_id=1, source_target_pairs={{0,4},{1,5},{4,8},{5,9},{8,12},{9,13},{12,14},{13,15},{14,10},{15,... | collective-permute-start | bytes 1572872 | tf_op jit(solution)/shard_map/ppermute | solution.py:244
  213.4 29.7 %copy-start.18 = (bf16[512,512]{1,0:T(8,128)(2,1)}, bf16[512,512]{1,0:T(8,128)(2,1)S(1)}, u32[]{:S(2)}) copy-start(bf16[512,512]{1,0:T(8,128)(2,1)S(1)} %collective-permute-done.6.refs_2_) | copy-start | bytes 1572868
  213.4 13.8 %collective-permute-start.8 = (bf16[512,512]{1,0:T(8,128)(2,1)S(1)}, bf16[512,512]{1,0:T(8,128)(2,1)S(1)}, u32[]{:S(2)}, u32[]{:S(2)}) collective-permute-start(bf16[512,512]{1,0:T(8,128)(2,1)S(1)} %collective-permute-done.6.refs_2_), channel_id=1, source_target_pairs={{0,2},{1,3},{4,0},{5,1},{8,4},{9,5},{12,8},{13,9},{14,12},{15,13},... | collective-permute-start | bytes 1572872 | tf_op jit(solution)/shard_map/ppermute | solution.py:247
  219.6 12.1 %collective-permute-start.9 = (bf16[512,512]{1,0:T(8,128)(2,1)S(1)}, bf16[512,512]{1,0:T(8,128)(2,1)S(1)}, u32[]{:S(2)}, u32[]{:S(2)}) collective-permute-start(bf16[512,512]{1,0:T(8,128)(2,1)S(1)} %collective-permute-done.7.refs_3_), channel_id=1, source_target_pairs={{0,4},{1,5},{4,8},{5,9},{8,12},{9,13},{12,14},{13,15},{14,10},{15,... | collective-permute-start | bytes 1572872 | tf_op jit(solution)/shard_map/ppermute | solution.py:244
  227.2 15.9 %copy-start.20 = (bf16[512,512]{1,0:T(8,128)(2,1)}, bf16[512,512]{1,0:T(8,128)(2,1)S(1)}, u32[]{:S(2)}) copy-start(bf16[512,512]{1,0:T(8,128)(2,1)S(1)} %collective-permute-done.8.refs_4_) | copy-start | bytes 1572868
  227.2 13.0 %collective-permute-start.10 = (bf16[512,512]{1,0:T(8,128)(2,1)S(1)}, bf16[512,512]{1,0:T(8,128)(2,1)S(1)}, u32[]{:S(2)}, u32[]{:S(2)}) collective-permute-start(bf16[512,512]{1,0:T(8,128)(2,1)S(1)} %collective-permute-done.8.refs_4_), channel_id=1, source_target_pairs={{0,2},{1,3},{4,0},{5,1},{8,4},{9,5},{12,8},{13,9},{14,12},{15,13},... | collective-permute-start | bytes 1572872 | tf_op jit(solution)/shard_map/ppermute | solution.py:247
  231.7 11.4 %collective-permute-start.11 = (bf16[512,512]{1,0:T(8,128)(2,1)S(1)}, bf16[512,512]{1,0:T(8,128)(2,1)}, u32[]{:S(2)}, u32[]{:S(2)}) collective-permute-start(bf16[512,512]{1,0:T(8,128)(2,1)S(1)} %collective-permute-done.9.refs_5_), channel_id=1, source_target_pairs={{0,4},{1,5},{4,8},{5,9},{8,12},{9,13},{12,14},{13,15},{14,10},{15,... | collective-permute-start | bytes 1572872 | tf_op jit(solution)/shard_map/ppermute | solution.py:244
  259.5 47.9 %all-to-all-start.3 = ((bf16[8,256,512]{2,1,0:T(8,128)(2,1)}), bf16[8,256,512]{2,1,0:T(8,128)(2,1)S(1)}, u32[]{:S(2)}, u32[]{:S(2)}) async-start(bf16[8,256,512]{2,1,0:T(8,128)(2,1)} %bitcast.62), calls=%async_computation.3 | async-start | bytes 4194304 | tf_op jit(solution)/shard_map/all_to_all | solution.py:289
  308.7 85.8 %all-to-all-start.1 = ((bf16[8,256,512]{2,1,0:T(8,128)(2,1)}), bf16[8,256,512]{2,1,0:T(8,128)(2,1)S(1)}, u32[]{:S(2)}, u32[]{:S(2)}) async-start(bf16[8,256,512]{2,1,0:T(8,128)(2,1)} %bitcast.61), calls=%async_computation.1 | async-start | bytes 4194304 | tf_op jit(solution)/shard_map/all_to_all | solution.py:289
  324.3 50.2 %copy-start.13 = (bf16[512,256]{1,0:T(8,128)(2,1)}, bf16[512,256]{1,0:T(8,128)(2,1)S(1)}, u32[]{:S(2)}) copy-start(bf16[512,256]{1,0:T(8,128)(2,1)S(1)} %get-tuple-element.14.refs_1_) | copy-start | bytes 786436
  324.3 42.1 %collective-permute-start.21 = (bf16[512,256]{1,0:T(8,128)(2,1)}, bf16[512,256]{1,0:T(8,128)(2,1)}, u32[]{:S(2)}, u32[]{:S(2)}) collective-permute-start(bf16[512,256]{1,0:T(8,128)(2,1)} %get-tuple-element.13.refs_2_), channel_id=1, source_target_pairs={{0,2},{1,3},{2,4},{3,5},{4,6},{5,7},{6,8},{7,9},{8,10},{9,11},{10,... | collective-permute-start | bytes 786440 | tf_op jit(solution)/shard_map/ppermute | solution.py:386
  368.2 16.6 %copy-start.37 = (s32[8192]{0:T(1024)S(1)}, s32[8192]{0:T(1024)}, u32[]{:S(2)}) copy-start(s32[8192]{0:T(1024)} %param.10) | copy-start | bytes 98308
  374.5 19.3 %collective-permute-start.23 = (bf16[512,512]{1,0:T(8,128)(2,1)}, bf16[512,512]{1,0:T(8,128)(2,1)}, u32[]{:S(2)}, u32[]{:S(2)}) collective-permute-start(bf16[512,512]{1,0:T(8,128)(2,1)} %shard_map.94), channel_id=1, source_target_pairs={{0,16},{16,0},{1,17},{17,1},{2,18},{18,2},{3,19},{19,3},{4,20},{20... | collective-permute-start | bytes 1572872 | tf_op jit(solution)/shard_map/ppermute | solution.py:286
  379.2 14.0 %copy-start.9 = (bf16[512,256]{1,0:T(8,128)(2,1)}, bf16[512,256]{1,0:T(8,128)(2,1)S(1)}, u32[]{:S(2)}) copy-start(bf16[512,256]{1,0:T(8,128)(2,1)S(1)} %get-tuple-element.11.refs_2_) | copy-start | bytes 786436
  379.2 14.5 %collective-permute-start.17 = (bf16[512,256]{1,0:T(8,128)(2,1)S(1)}, bf16[512,256]{1,0:T(8,128)(2,1)S(1)}, u32[]{:S(2)}, u32[]{:S(2)}) collective-permute-start(bf16[512,256]{1,0:T(8,128)(2,1)S(1)} %get-tuple-element.11.refs_2_), channel_id=1, source_target_pairs={{0,2},{1,3},{2,4},{3,5},{4,6},{5,7},{6,8},{7,9},{8,10},{9,11},{10,... | collective-permute-start | bytes 786440 | tf_op jit(solution)/shard_map/ppermute | solution.py:386
  393.2 13.6 %collective-permute-start.22 = (bf16[512,512]{1,0:T(8,128)(2,1)}, bf16[512,512]{1,0:T(8,128)(2,1)}, u32[]{:S(2)}, u32[]{:S(2)}) collective-permute-start(bf16[512,512]{1,0:T(8,128)(2,1)} %shard_map.93), channel_id=1, source_target_pairs={{0,16},{16,0},{1,17},{17,1},{2,18},{18,2},{3,19},{19,3},{4,20},{20... | collective-permute-start | bytes 1572872 | tf_op jit(solution)/shard_map/ppermute | solution.py:286
  393.8 13.1 %collective-permute-start.24 = (bf16[512,512]{1,0:T(8,128)(2,1)}, bf16[512,512]{1,0:T(8,128)(2,1)}, u32[]{:S(2)}, u32[]{:S(2)}) collective-permute-start(bf16[512,512]{1,0:T(8,128)(2,1)} %collective-permute-done.23), channel_id=1, source_target_pairs={{0,1},{1,0},{2,3},{3,2},{4,5},{5,4},{6,7},{7,6},{8,9},{9,8},{10,11... | collective-permute-start | bytes 1572872 | tf_op jit(solution)/shard_map/ppermute | solution.py:283
  401.0 13.8 %collective-permute-start.18 = (bf16[512,512]{1,0:T(8,128)(2,1)S(1)}, bf16[512,512]{1,0:T(8,128)(2,1)S(1)}, u32[]{:S(2)}, u32[]{:S(2)}) collective-permute-start(bf16[512,512]{1,0:T(8,128)(2,1)S(1)} %shard_map.87), channel_id=1, source_target_pairs={{0,1},{1,0},{2,3},{3,2},{4,5},{5,4},{6,7},{7,6},{8,9},{9,8},{10,11... | collective-permute-start | bytes 1572872 | tf_op jit(solution)/shard_map/ppermute | solution.py:283
  (24 other events, 82.6 us)
